TPU v7x, 256 devices: a whole 4x4x8 slice. The times are simulated.
256 devices in a mesh: gx: 8 (over z), gy: 8 (over x, y_hi), gz: 4 (over y_lo, core).
Axes of the slice: x: 4, y: 4 (y_hi: 2, y_lo: 2; y = y_hi * 2 + y_lo), z: 8, core: 2. Of those that a mesh axis runs over, the one named last changes fastest.
Arguments:
- adjoint_in: float32 [14, 128, 128, 512], P(None, 'gx', 'gy', 'gz'), may hold values from -6 to 6
- velocity: float32 [3, 128, 128, 512], P(None, 'gx', 'gy', 'gz'), may hold values from -6 to 6
- viscosity: float32 [128, 128, 512], P('gx', 'gy', 'gz'), may hold values from 0.2 to 2
- rate: float32 [128, 128, 512], P('gx', 'gy', 'gz'), may hold values from 0.1 to 1
- chemistry: float32 [14, 14], replicated, may hold values from -1.5 to 1.5
- stencil_x: float32 [2, 16, 24], replicated, may hold values from -0.875 to 0.875
- stencil_y: float32 [2, 16, 24], replicated, may hold values from -0.875 to 0.875
- stencil_z: float32 [2, 128, 136], replicated, may hold values from -0.375 to 0.375
- sensitivity: float32 [128, 128, 512], P(None, 'gx', 'gz'), may hold values from -0.03125 to 0.03125
- patch_ids: int32 [8, 8, 4], P('gx', 'gy', 'gz'), may hold values from 0 to 255
Outputs:
- adjoint_out: float32 [14, 128, 128, 512], P(None, 'gx', 'gy', 'gz')
- shape_grad: float32 [256, 128], P(('gx', 'gy', 'gz'))
All inputs are finite; a program needn't handle non-finite values.
Results may differ from a plain program's by a relative error of at most 0.000078.
Values sent between devices are 32-bit elements; how exact they have to be, the bound alone decides.
No kernel may reach another device: no remote copies, remote signals or barrier semaphores. Data moves between devices by JAX's collectives and lax.ppermute only.
A program may use at most 128 MiB of HBM per device.

v0:
```python
import jax
import jax.numpy as jnp
from jax import lax
from jax.sharding import PartitionSpec as P

PATCH_DEV = 1


section_step = 0.5
hydrogen = 5
highest = lax.Precision.HIGHEST


def extended(x, sides, width):
    for axis, dim in sides:
        size, length = (lax.axis_size(axis), x.shape[dim])
        up = [(i, (i + 1) % size) for i in range(size - 1)]
        down = [(j, i) for i, j in up]
        last = lax.slice_in_dim(x, length - width, length, axis=dim)
        leading = lax.slice_in_dim(x, 0, width, axis=dim)
        before = lax.ppermute(last, axis, up)
        after = lax.ppermute(leading, axis, down)
        x = jnp.concatenate([before, x, after], axis=dim)
    return x


def apply_dir(padded_dir, components, velocity_row, stencil, form):
    adjoint_pad = padded_dir[:components]
    advected = -padded_dir[components + velocity_row] * adjoint_pad
    diffused = padded_dir[components + 3] * adjoint_pad
    first = jnp.einsum(form, stencil[0], advected, precision=highest)
    second = jnp.einsum(form, stencil[1], diffused, precision=highest)
    return first + second


def shards(
    adjoint_in,
    velocity,
    viscosity,
    rate,
    chemistry,
    stencil_x,
    stencil_y,
    stencil_z,
    sensitivity,
    patch_ids,
):
    components = adjoint_in.shape[0]
    stacked = jnp.concatenate([adjoint_in, velocity, viscosity[None]], axis=0)
    padded = extended(stacked, (("gx", 1), ("gy", 2), ("gz", 3)), 4)
    transport = apply_dir(padded[:, :, 4:-4, 4:-4], components, 0, stencil_x, "ij,vjyz->viyz")
    transport = transport + apply_dir(
        padded[:, 4:-4, :, 4:-4], components, 1, stencil_y, "ij,vxjz->vxiz"
    )
    transport = transport + apply_dir(
        padded[:, 4:-4, 4:-4, :], components, 2, stencil_z, "ij,vxyj->vxyi"
    )
    reacting = jnp.tensordot(chemistry.T, rate[None] * adjoint_in, axes=1, precision=highest)
    adjoint_out = adjoint_in + section_step * (transport + reacting)
    partial_value = jnp.einsum("pxz,xyz->p", sensitivity, adjoint_in[hydrogen], precision=highest)
    patch_id = patch_ids.reshape(())
    devices_all = lax.axis_size("gx") * lax.axis_size("gy") * lax.axis_size("gz")
    patch_total = PATCH_DEV * devices_all
    selector = (jnp.arange(patch_total, dtype=jnp.int32) == patch_id).astype(jnp.float32)
    contrib = selector[:, None] * partial_value[None, :]
    owned = lax.psum_scatter(contrib, ("gx", "gy", "gz"), scatter_dimension=0, tiled=True)
    shape_grad = section_step * owned
    return (adjoint_out, shape_grad)


def solution(mesh):
    return jax.shard_map(
        shards,
        mesh=mesh,
        in_specs=(
            P(None, "gx", "gy", "gz"),
            P(None, "gx", "gy", "gz"),
            P("gx", "gy", "gz"),
            P("gx", "gy", "gz"),
            P(),
            P(),
            P(),
            P(),
            P(None, "gx", "gz"),
            P("gx", "gy", "gz"),
        ),
        out_specs=(P(None, "gx", "gy", "gz"), P(("gx", "gy", "gz"), None)),
        check_vma=False,
    )
```

profile of v0, /device:TPU:1, one launch (start us, length us, event | category | flops | bytes accessed | tf_op | source)
XLA Modules:
  0.0 397.2 jit_solution(11175599716885429453)
XLA Ops:
  7.2 0.0 copy-start
  7.2 0.0 copy-start.2
  7.2 0.0 all-reduce.3.cloned.1.call-start
  7.2 2.6 pad_maximum_fusion.7
  9.8 4.5 %collective-permute-start = (f32[18,4,16,128]{3,2,1,0:T(8,128)}, f32[18,4,16,128]{3,2,1,0:T(8,128)S(1)}, u32[]{:S(2)}, u32[]{:S(2)}) collective-permute-start(f32[18,4,16,128]{3,2,1,0:T(8,128)} %get-tuple-element.22), channel_id=1, source_target_pairs={{0,32},{32,64},{64,96},{96,128},{128,160},{160,192},{192,224},{1,3... | collective-permute-start | bytes 1769480 | tf_op jit(solution)/shard_map/ppermute | solution.py:21
  14.4 1.3 collective-permute-start.1
  15.7 0.0 copy-done.2
  16.4 0.0 copy-done
  16.4 1.0 convolution_bitcast_fusion
  17.4 0.8 broadcast_multiply_fusion.1
  18.2 0.0 all-reduce.3.cloned.1.call-update
  18.2 1.0 broadcast_multiply_fusion
  19.2 0.0 copy-done.17
  19.2 0.0 copy-start.5
  19.2 0.0 copy-start.13
  19.3 4.5 %fusion.14 = f32[16,16,128,14]{2,3,1,0:T(8,128)} fusion(f32[14,16,16,128]{3,2,1,0:T(8,128)S(1)} %broadcast_multiply_fusion, f32[14,14]{1,0:T(8,128)S(1)} %copy-done.17), kind=kOutput, calls=%fused_computation.21 | convolution fusion | flops 77070336 | bytes 3670800 | tf_op jit(solution)/shard_map/dot_general | solution.py:58
  23.8 240.4 %all-reduce.3.cloned.1.call-done = f32[256,128]{1,0:T(8,128)} async-done(((f32[256,128]{1,0:T(8,128)}), f32[256,128]{1,0:T(8,128)}) %all-reduce.3.cloned.1.call-update) | async-done | bytes 131088
  264.2 1.2 dynamic-slice_multiply_fusion
  265.4 0.0 collective-permute-done
  265.4 0.0 collective-permute-done.1
  265.4 0.0 copy-done.5
  265.4 0.0 copy-done.13
  265.4 1.5 pad_maximum_fusion.4
  266.9 0.1 copy.45
  267.0 4.5 %collective-permute-start.2 = (f32[18,24,4,128]{3,1,2,0:T(8,128)S(1)}, f32[18,24,4,128]{3,1,2,0:T(8,128)S(1)}, u32[]{:S(2)}, u32[]{:S(2)}) collective-permute-start(f32[18,24,4,128]{3,1,2,0:T(8,128)S(1)} %copy.45), channel_id=1, source_target_pairs={{0,4},{4,8},{8,12},{12,16},{16,20},{20,24},{24,28},{1,5},{5,9},{9,... | collective-permute-start | bytes 2654216 | tf_op jit(solution)/shard_map/ppermute | solution.py:21
  271.5 0.1 copy.46
  271.6 1.8 collective-permute-start.3
  273.4 0.8 maximum_bitcast_fusion.1
  274.2 1.3 pad_maximum_fusion.2
  275.5 0.0 copy-start.15
  275.5 0.6 slice_multiply_fusion.2
  276.1 0.1 copy-done.15
  276.2 3.8 fusion.4
  280.0 3.8 fusion.6
  283.8 23.8 %collective-permute-done.2 = f32[18,24,4,128]{3,1,2,0:T(8,128)S(1)} collective-permute-done((f32[18,24,4,128]{3,1,2,0:T(8,128)S(1)}, f32[18,24,4,128]{3,1,2,0:T(8,128)S(1)}, u32[]{:S(2)}, u32[]{:S(2)}) %collective-permute-start.2) | collective-permute-done | bytes 884768 | tf_op jit(solution)/shard_map/ppermute | solution.py:21
  307.6 0.2 copy.47
  307.8 0.0 copy-start.6
  307.8 0.0 collective-permute-done.3
  307.8 0.2 copy.48
  308.1 0.7 copy-done.6
  308.7 1.0 copy-done.7
  309.7 3.8 pad_maximum_fusion.1
  313.5 5.9 %fusion.40 = (f32[18,24,24,4]{3,2,1,0:T(8,128)}, f32[18,24,24,4]{3,2,1,0:T(8,128)}) fusion(f32[18,24,24,128]{3,2,1,0:T(8,128)S(1)} %pad_maximum_fusion.1), kind=kLoop, calls=%fused_computation.65 | loop fusion | bytes 663552 | tf_op jit(solution)/shard_map/slice | solution.py:19
  319.5 5.3 %copy.51 = f32[18,24,24,4]{2,1,3,0:T(8,128)} copy(f32[18,24,24,4]{3,2,1,0:T(8,128)} %get-tuple-element.12) | data formatting | bytes 331776 | tf_op jit(solution)/shard_map/slice | solution.py:19
  324.7 4.8 %collective-permute-start.4 = (f32[18,24,24,4]{2,1,3,0:T(8,128)}, f32[18,24,24,4]{2,1,3,0:T(8,128)}, u32[]{:S(2)}, u32[]{:S(2)}) collective-permute-start(f32[18,24,24,4]{2,1,3,0:T(8,128)} %copy.51), channel_id=1, source_target_pairs={{0,1},{1,2},{2,3},{4,5},{5,6},{6,7},{8,9},{9,10},{10,11},{12,13},{... | collective-permute-start | bytes 497672 | tf_op jit(solution)/shard_map/ppermute | solution.py:21
  329.5 5.3 %copy.52 = f32[18,24,24,4]{2,1,3,0:T(8,128)} copy(f32[18,24,24,4]{3,2,1,0:T(8,128)} %get-tuple-element.13) | data formatting | bytes 331776 | tf_op jit(solution)/shard_map/slice | solution.py:20
  334.8 2.4 collective-permute-start.5
  337.2 0.9 fusion.25
  338.1 3.2 fusion.10
  341.3 3.2 fusion.8
  344.5 0.0 collective-permute-done.4
  344.5 5.2 %copy.53 = f32[18,24,24,4]{3,2,1,0:T(8,128)} copy(f32[18,24,24,4]{2,1,3,0:T(8,128)} %collective-permute-done.4) | data formatting | bytes 331776 | tf_op jit(solution)/shard_map/ppermute | solution.py:21
  349.7 0.0 collective-permute-done.5
  349.7 5.2 %copy.54 = f32[18,24,24,4]{3,2,1,0:T(8,128)} copy(f32[18,24,24,4]{2,1,3,0:T(8,128)} %collective-permute-done.5) | data formatting | bytes 331776 | tf_op jit(solution)/shard_map/ppermute | solution.py:22
  355.0 19.2 %pad_maximum_fusion = f32[18,24,24,136]{3,2,1,0:T(8,128)S(1)} fusion(f32[18,24,24,4]{3,2,1,0:T(8,128)} %copy.54, f32[18,24,4,128]{3,2,1,0:T(4,128)} %copy-done.7, f32[18,4,16,128]{3,2,1,0:T(8,128)} %collective-permute-done.1, f32[1,16,16,128]{3,2,1,0:T(8,128)S(1)} %bitcast.86, f32[3,16,16,128]{3,2,1,0:T(8,128)S(1)} %copy-done.5, ...), kind=kLoop, calls=%fused_computation | loop fusion | flops 11280384 | bytes 11280384 | tf_op jit(solution)/shard_map/concatenate | solution.py:23
  374.2 0.1 fusion.24
  374.2 0.0 copy-start.14
  374.3 0.0 copy-start.12
  374.3 1.2 slice_multiply_fusion.1
  375.5 5.0 %fusion = f32[14,16,16,128]{3,1,2,0:T(8,128)S(1)} fusion(f32[14,16,16,136]{3,2,1,0:T(8,128)S(1)} %get-tuple-element.9, f32[2,128,136]{1,2,0:T(8,128)S(1)} %copy-done.14), kind=kOutput, calls=%fused_computation.2 | convolution fusion | flops 748683264 | bytes 5574656 | tf_op jit(solution)/shard_map/ij,vxyj->vxyi/dot_general | solution.py:32
  380.5 0.0 copy-start.1
  380.5 7.8 %fusion.17 = f32[14,16,16,128]{3,1,2,0:T(8,128)S(1)} fusion(f32[14,16,16,128]{3,2,1,0:T(8,128)S(1)} %copy-done.2, f32[16,16,128,14]{2,3,1,0:T(8,128)S(1)} %copy-done.8, f32[14,16,128,16]{2,3,1,0:T(8,128)S(1)} %copy-done.12, f32[14,16,128,16]{2,3,1,0:T(8,128)S(1)} %copy-done.11, f32[14,16,16,128]{3,1,2,0:T(8,128)S(1)} %fusion, ...), kind=kOutput, calls=%fused_computation.25 | convolution fusion | flops 752353280 | bytes 18681856 | tf_op jit(solution)/shard_map/ij,vxyj->vxyi/dot_general | solution.py:31
  388.3 1.8 copy.61
  390.1 0.0 copy-done.1
  (20 shorter events, 0.1 us)
Async XLA Ops:
  7.2 9.2 %copy-start = (f32[128,16,128]{2,1,0:T(8,128)S(1)}, f32[128,16,128]{2,1,0:T(8,128)}, u32[]{:S(2)}) copy-start(f32[128,16,128]{2,1,0:T(8,128)} %param.18) | copy-start | bytes 3145732
  7.2 8.5 %copy-start.2 = (f32[14,16,16,128]{3,2,1,0:T(8,128)S(1)}, f32[14,16,16,128]{3,2,1,0:T(8,128)}, u32[]{:S(2)}) copy-start(f32[14,16,16,128]{3,2,1,0:T(8,128)} %param.10) | copy-start | bytes 5505028
  7.2 257.0 %all-reduce.3.cloned.1.call-start = ((), (), s32[]{:S(2)}) async-start(), calls=%async_computation | async-start | bytes 262144
  9.8 9.4 %copy-start.17 = (f32[14,14]{1,0:T(8,128)S(1)}, f32[14,14]{1,0:T(8,128)}, u32[]{:S(2)}) copy-start(f32[14,14]{1,0:T(8,128)} %param.14) | copy-start | bytes 2356
  9.8 255.6 %collective-permute-start = (f32[18,4,16,128]{3,2,1,0:T(8,128)}, f32[18,4,16,128]{3,2,1,0:T(8,128)S(1)}, u32[]{:S(2)}, u32[]{:S(2)}) collective-permute-start(f32[18,4,16,128]{3,2,1,0:T(8,128)} %get-tuple-element.22), channel_id=1, source_target_pairs={{0,32},{32,64},{64,96},{96,128},{128,160},{160,192},{192,224},{1,3... | collective-permute-start | bytes 1769480 | tf_op jit(solution)/shard_map/ppermute | solution.py:21
  14.4 251.0 %collective-permute-start.1 = (f32[18,4,16,128]{3,2,1,0:T(8,128)}, f32[18,4,16,128]{3,2,1,0:T(8,128)}, u32[]{:S(2)}, u32[]{:S(2)}) collective-permute-start(f32[18,4,16,128]{3,2,1,0:T(8,128)} %get-tuple-element.23), channel_id=1, source_target_pairs={{32,0},{64,32},{96,64},{128,96},{160,128},{192,160},{224,192},{33,... | collective-permute-start | bytes 1769480 | tf_op jit(solution)/shard_map/ppermute | solution.py:22
  19.2 246.2 %copy-start.5 = (f32[3,16,16,128]{3,2,1,0:T(8,128)S(1)}, f32[3,16,16,128]{3,2,1,0:T(8,128)}, u32[]{:S(2)}) copy-start(f32[3,16,16,128]{3,2,1,0:T(8,128)} %param.11) | copy-start | bytes 1179652
  19.2 246.2 %copy-start.13 = (f32[16,16,128]{2,1,0:T(8,128)S(1)}, f32[16,16,128]{2,1,0:T(8,128)}, u32[]{:S(2)}) copy-start(f32[16,16,128]{2,1,0:T(8,128)} %param.12) | copy-start | bytes 393220
  267.0 40.6 %collective-permute-start.2 = (f32[18,24,4,128]{3,1,2,0:T(8,128)S(1)}, f32[18,24,4,128]{3,1,2,0:T(8,128)S(1)}, u32[]{:S(2)}, u32[]{:S(2)}) collective-permute-start(f32[18,24,4,128]{3,1,2,0:T(8,128)S(1)} %copy.45), channel_id=1, source_target_pairs={{0,4},{4,8},{8,12},{12,16},{16,20},{20,24},{24,28},{1,5},{5,9},{9,... | collective-permute-start | bytes 2654216 | tf_op jit(solution)/shard_map/ppermute | solution.py:21
  271.6 36.3 %collective-permute-start.3 = (f32[18,24,4,128]{3,1,2,0:T(8,128)S(1)}, f32[18,24,4,128]{3,1,2,0:T(8,128)S(1)}, u32[]{:S(2)}, u32[]{:S(2)}) collective-permute-start(f32[18,24,4,128]{3,1,2,0:T(8,128)S(1)} %copy.46), channel_id=1, source_target_pairs={{4,0},{8,4},{12,8},{16,12},{20,16},{24,20},{28,24},{5,1},{9,5},{13... | collective-permute-start | bytes 2654216 | tf_op jit(solution)/shard_map/ppermute | solution.py:22
  275.5 0.7 copy-start.15
  307.8 0.9 copy-start.6
  308.7 1.0 copy-start.7
  313.5 6.0 %copy-start.3 = (f32[18,24,24,128]{3,2,1,0:T(8,128)}, f32[18,24,24,128]{3,2,1,0:T(8,128)S(1)}, u32[]{:S(2)}) copy-start(f32[18,24,24,128]{3,2,1,0:T(8,128)S(1)} %pad_maximum_fusion.1) | copy-start | bytes 15925252
  324.7 19.8 %collective-permute-start.4 = (f32[18,24,24,4]{2,1,3,0:T(8,128)}, f32[18,24,24,4]{2,1,3,0:T(8,128)}, u32[]{:S(2)}, u32[]{:S(2)}) collective-permute-start(f32[18,24,24,4]{2,1,3,0:T(8,128)} %copy.51), channel_id=1, source_target_pairs={{0,1},{1,2},{2,3},{4,5},{5,6},{6,7},{8,9},{9,10},{10,11},{12,13},{... | collective-permute-start | bytes 497672 | tf_op jit(solution)/shard_map/ppermute | solution.py:21
  334.8 3.3 copy-start.4
  334.8 3.3 copy-start.16
  334.8 14.9 %collective-permute-start.5 = (f32[18,24,24,4]{2,1,3,0:T(8,128)}, f32[18,24,24,4]{2,1,3,0:T(8,128)}, u32[]{:S(2)}, u32[]{:S(2)}) collective-permute-start(f32[18,24,24,4]{2,1,3,0:T(8,128)} %copy.52), channel_id=1, source_target_pairs={{1,0},{2,1},{3,2},{5,4},{6,5},{7,6},{9,8},{10,9},{11,10},{13,12},{... | collective-permute-start | bytes 497672 | tf_op jit(solution)/shard_map/ppermute | solution.py:22
  374.2 1.2 copy-start.14
  374.2 6.2 %copy-start.10 = (f32[14,16,128,16]{2,3,1,0:T(8,128)S(1)}, f32[14,16,128,16]{2,3,1,0:T(8,128)}, u32[]{:S(2)}) copy-start(f32[14,16,128,16]{2,3,1,0:T(8,128)} %fusion.6) | copy-start | bytes 5505028
  374.3 6.2 %copy-start.11 = (f32[14,16,128,16]{2,3,1,0:T(8,128)S(1)}, f32[14,16,128,16]{2,3,1,0:T(8,128)}, u32[]{:S(2)}) copy-start(f32[14,16,128,16]{2,3,1,0:T(8,128)} %fusion.10) | copy-start | bytes 5505028
  374.3 6.2 %copy-start.12 = (f32[14,16,128,16]{2,3,1,0:T(8,128)S(1)}, f32[14,16,128,16]{2,3,1,0:T(8,128)}, u32[]{:S(2)}) copy-start(f32[14,16,128,16]{2,3,1,0:T(8,128)} %fusion.8) | copy-start | bytes 5505028
  375.5 5.0 %copy-start.8 = (f32[16,16,128,14]{2,3,1,0:T(8,128)S(1)}, f32[16,16,128,14]{2,3,1,0:T(8,128)}, u32[]{:S(2)}) copy-start(f32[16,16,128,14]{2,3,1,0:T(8,128)} %fusion.14) | copy-start | bytes 5505028
  375.5 5.0 %copy-start.9 = (f32[14,16,128,16]{2,3,1,0:T(8,128)S(1)}, f32[14,16,128,16]{2,3,1,0:T(8,128)}, u32[]{:S(2)}) copy-start(f32[14,16,128,16]{2,3,1,0:T(8,128)} %fusion.4) | copy-start | bytes 5505028
  380.5 9.6 %copy-start.1 = (f32[128,16,128]{2,1,0:T(8,128)S(1)}, f32[128,16,128]{2,1,0:T(8,128)}, u32[]{:S(2)}) copy-start(f32[128,16,128]{2,1,0:T(8,128)} %param.18) | copy-start | bytes 3145732
Sparse Core Ops, SparseCore 0:
  18.3 245.8 all-reduce.2
where the time goes:
time: 403 us; the launch traced here: 397 us
  waiting for transfers between devices  264 us (66%)
  other arithmetic  34.9 us (9%)
  matrix products  32.3 us (8%)
  local copies, waits for them, and re-layouts  31.1 us (8%)
  starting transfers between devices  19.3 us (5%)
  between operations  15.3 us (4%)
    unnamed x2, waiting for transfers between devices  240 us
    concatenate x3, other arithmetic, extended(): x = jnp.concatenate([before, x, after], axis=dim)  24.3 us
    ppermute x3, waiting for transfers between devices, extended(): before = lax.ppermute(last, axis, up)  23.8 us
    dot_general x3, matrix products, apply_dir(): first = jnp.einsum(form, stencil[0], advected, precision=highest)  14.8 us
    ppermute x3, starting transfers between devices, extended(): before = lax.ppermute(last, axis, up)  13.8 us
    dot_general x3, matrix products, apply_dir(): second = jnp.einsum(form, stencil[1], diffused, precision=highest)  12 us
    slice x3, local copies, waits for them, and re-layouts, extended(): last = lax.slice_in_dim(x, length - width, length, axis=dim)  11.3 us
  transfers between devices with their start and end apart: 7, of which 2 were waited for; matrix products, arithmetic and copies ran while one was open for 9% of the time, Pallas kernels for 0%

commit v1 on v0

v1 whole, which is shorter than its diff:
```python
import functools

import jax
import jax.numpy as jnp
from jax import lax
from jax.experimental import pallas as pl
from jax.experimental.pallas import tpu as pltpu
from jax.sharding import PartitionSpec as P

section_step = 0.5
hydrogen = 5
highest = lax.Precision.HIGHEST
AXES = ("gx", "gy", "gz")
f32, bf16, i32 = jnp.float32, jnp.bfloat16, jnp.int32


def swap(a, b, axis):
    n = lax.axis_size(axis)
    plan_a = [(i, i ^ 1) for i in range(n)]
    plan_b = [(i, (i - 1) % n if i % 2 == 0 else (i + 1) % n) for i in range(n)]
    return lax.ppermute(a, axis, plan_a), lax.ppermute(b, axis, plan_b)


def is_even(axis):
    return lax.rem(lax.axis_index(axis), 2) == 0


def iota(shape, dim):
    return lax.broadcasted_iota(i32, shape, dim)


def split(x):
    hi = x.astype(bf16)
    return hi, (x - hi.astype(f32)).astype(bf16)


def mm(a, b):
    return jnp.dot(a, b, preferred_element_type=f32)


CHUNKS = ((0, 4), (4, 8), (8, 12), (12, 16))


def pack_xy(adj, vel, visc, gya, gyb, gxa, gxb, buf, oa, ob, sem_in, sem_x, sem_out):
    nv = adj.shape[0]
    even_x, even_y = is_even("gx"), is_even("gy")
    ins = []
    for k, (c0, c1) in enumerate(CHUNKS):
        top = min(c1, nv)
        group = [pltpu.make_async_copy(adj.at[c0:top], buf.at[c0:top], sem_in.at[k, 0])]
        if c1 > nv:
            group.append(pltpu.make_async_copy(vel.at[1], buf.at[nv], sem_in.at[k, 1]))
            group.append(pltpu.make_async_copy(visc, buf.at[nv + 1], sem_in.at[k, 2]))
        for c in group:
            c.start()
        ins.append(group)
    xs = []
    last = adj.shape[1] - 4
    for side, out in enumerate((gxa, gxb)):
        want_last = even_x if side == 0 else jnp.logical_not(even_x)
        at = pl.ds(jnp.where(want_last, last, 0), 4)
        xs.append(pltpu.make_async_copy(adj.at[:, at], out.at[0:nv], sem_x.at[side, 0]))
        xs.append(pltpu.make_async_copy(vel.at[0, at], out.at[nv], sem_x.at[side, 1]))
        xs.append(pltpu.make_async_copy(visc.at[at], out.at[nv + 1], sem_x.at[side, 2]))
    for c in xs:
        c.start()
    outs = []
    for k, (c0, c1) in enumerate(CHUNKS):
        for c in ins[k]:
            c.wait()
        first = jnp.concatenate([buf[c0:c1, 8:16, 0:4, :], buf[c0:c1, 0:8, 0:4, :]], axis=2)
        final = jnp.concatenate([buf[c0:c1, 8:16, 12:16, :], buf[c0:c1, 0:8, 12:16, :]], axis=2)
        oa[c0:c1] = jnp.where(even_y, final, first)
        ob[c0:c1] = jnp.where(even_y, first, final)
        for side, (src, dst) in enumerate(((oa, gya), (ob, gyb))):
            c = pltpu.make_async_copy(src.at[c0:c1], dst.at[c0:c1], sem_out.at[side, k])
            c.start()
            outs.append(c)
    for c in xs + outs:
        c.wait()


def call_pack_xy(adj, vel, visc):
    nv = adj.shape[0]
    gy = jax.ShapeDtypeStruct((nv + 2, 8, 8, 128), f32)
    gx = jax.ShapeDtypeStruct((nv + 2, 4, 16, 128), f32)
    anyspec = pl.BlockSpec(memory_space=pl.ANY)
    return pl.pallas_call(
        pack_xy,
        out_shape=(gy, gy, gx, gx),
        in_specs=[anyspec] * 3,
        out_specs=(anyspec,) * 4,
        scratch_shapes=[
            pltpu.VMEM((nv + 2, 16, 16, 128), f32),
            pltpu.VMEM((nv + 2, 8, 8, 128), f32),
            pltpu.VMEM((nv + 2, 8, 8, 128), f32),
            pltpu.SemaphoreType.DMA((4, 3)),
            pltpu.SemaphoreType.DMA((2, 3)),
            pltpu.SemaphoreType.DMA((2, 4)),
        ],
        compiler_params=pltpu.CompilerParams(vmem_limit_bytes=24 << 20),
        cost_estimate=pl.CostEstimate(flops=0, bytes_accessed=6 << 20, transcendentals=0),
        name="pack_xy",
    )(adj, vel, visc)


def pack_z(ids, adj, vel, visc, sens, gza, gzb, contrib):
    nv = adj.shape[0]
    lane = iota((256, 128), 1)
    face = jnp.zeros((256, 128), f32)
    for c in range(nv + 2):
        field = adj[c] if c < nv else (vel[0] if c == nv else visc[...])
        face = jnp.where(lane >> 3 == c, pltpu.roll(field, (8 * c + 4) % 128, 1), face)
    low = (iota((128, 128), 1) & 4) == 0
    top, bottom = face[:128], face[128:]
    finals = jnp.where(low, top, pltpu.roll(bottom, 4, 1))
    firsts = jnp.where(low, pltpu.roll(top, 124, 1), bottom)
    even = is_even("gz")
    gza[...] = jnp.where(even, finals, firsts)
    gzb[...] = jnp.where(even, firsts, finals)
    column = jnp.sum(adj[hydrogen].reshape(16, 16, 128), axis=1)
    terms = jnp.sum(sens[...] * column[None], axis=1)
    partial = jnp.sum(terms.T, axis=0, keepdims=True)
    owner = iota(contrib.shape, 0) == ids[0]
    contrib[...] = jnp.where(owner, jnp.broadcast_to(partial, contrib.shape), 0.0)


def call_pack_z(ids, adj, vel, visc, sens, patches):
    nv = adj.shape[0]
    face = jax.ShapeDtypeStruct((128, 128), f32)
    vm = pl.BlockSpec(memory_space=pltpu.VMEM)
    return pl.pallas_call(
        pack_z,
        grid=(1,),
        out_shape=(face, face, jax.ShapeDtypeStruct((patches, 128), f32)),
        in_specs=[
            pl.BlockSpec(memory_space=pltpu.SMEM),
            pl.BlockSpec((nv, 256, 128), lambda i: (0, 0, 0)),
            pl.BlockSpec((1, 256, 128), lambda i: (2, 0, 0)),
            vm,
            vm,
        ],
        out_specs=(vm, vm, vm),
        compiler_params=pltpu.CompilerParams(vmem_limit_bytes=24 << 20),
        cost_estimate=pl.CostEstimate(flops=1 << 20, bytes_accessed=4 << 20, transcendentals=0),
        name="pack_z",
    )(ids, adj, vel, visc, sens)


def halo_columns(axis, in_a, j, length):
    index, n = lax.axis_index(axis), lax.axis_size(axis)
    even = is_even(axis)
    after = jnp.where(even, in_a, 1 - in_a) == 1
    col = jnp.where(after, length + 4 + j, j)
    has_after = jnp.where(index < n - 1, 1, 0)
    has_before = jnp.where(index > 0, 1, 0)
    return jnp.where(jnp.where(after, has_after, has_before) == 1, col, -1)


def build_matrices(sx, sy, m_loc, m_halo_hi, m_halo_lo):
    rows, k16 = iota((256, 16), 0), iota((256, 16), 1)
    pick_x = (rows >> 4 == k16).astype(f32)
    pick_y = (rows & 15 == k16).astype(f32)
    c_loc, k_loc = iota((24, 256), 1), iota((24, 256), 0)
    c_halo, k_halo = iota((24, 128), 1), iota((24, 128), 0)
    in_a = jnp.where(c_halo < 64, 1, 0)
    col_x = halo_columns("gx", in_a, (c_halo & 63) >> 4, 16)
    col_y = halo_columns("gy", in_a, c_halo & 3, 16)
    cols_x = jnp.concatenate([k_loc == 4 + (c_loc >> 4), k_halo == col_x], axis=1).astype(f32)
    cols_y = jnp.concatenate([k_loc == 4 + (c_loc & 15), k_halo == col_y], axis=1).astype(f32)
    dot = functools.partial(jnp.dot, precision=highest, preferred_element_type=f32)
    r, c = iota((256, 256), 0), iota((256, 256), 1)
    same_y, same_x = (r & 15) == (c & 15), (r >> 4) == (c >> 4)
    rh, ch = iota((256, 128), 0), iota((256, 128), 1)
    same_yh = (rh & 15) == (ch & 15)
    x_of = ((ch & 63) >> 3) + jnp.where((ch & 7) >= 4, 0, 8)
    same_xh = (rh >> 4) == x_of
    full = []
    for f, scale in ((0, -section_step), (1, section_step)):
        tx = dot(dot(pick_x, sx[f] * scale), cols_x)
        ty = dot(dot(pick_y, sy[f] * scale), cols_y)
        full.append((jnp.where(same_y, tx[:, :256], 0.0), jnp.where(same_x, ty[:, :256], 0.0)))
        for part, (mask, t) in enumerate(((same_yh, tx), (same_xh, ty))):
            hi, lo = split(jnp.where(mask, t[:, 256:], 0.0))
            at = (2 * part + f) * 128
            m_halo_hi[:, at : at + 128] = hi
            m_halo_lo[:, at : at + 128] = lo
    for g, m in enumerate((full[0][0], full[0][1], full[1][0] + full[1][1])):
        hi, lo = split(m)
        m_loc[:, g * 256 : g * 256 + 256] = hi
        m_loc[:, 768 + g * 256 : 768 + g * 256 + 256] = lo


def interior(
    chem, adj, vel, visc, rate, sx, sy, szt, out, m_halo_hi, m_halo_lo, tile_hi, tile_lo, m_loc, wz
):
    nv = adj.shape[0]
    build_matrices(sx, sy, m_loc, m_halo_hi, m_halo_lo)
    index, n = lax.axis_index("gz"), lax.axis_size("gz")
    before = jnp.where(index > 0, 1.0, 0.0)
    after = jnp.where(index < n - 1, 1.0, 0.0)
    for f, scale in ((0, -section_step), (1, section_step)):
        hi, lo = split(szt[f, 4:132, :] * scale)
        wz[f * 128 : f * 128 + 128, 0:128] = hi
        wz[f * 128 : f * 128 + 128, 128:256] = lo
        ends = jnp.concatenate(
            [szt[f, 0:4, :] * (scale * before), szt[f, 132:136, :] * (scale * after)], axis=0
        )
        hi, lo = split(jnp.concatenate([ends] * 16, axis=0))
        tile_hi[f * 128 : f * 128 + 128, :] = hi
        tile_lo[f * 128 : f * 128 + 128, :] = lo

    def pair(i, carry):
        highs, lows, zs = [], [], []
        for k in range(2):
            a = adj[2 * i + k]
            parts = [split(vel[0] * a), split(vel[1] * a), split(visc[...] * a)]
            highs.append(jnp.concatenate([p[0] for p in parts], axis=0))
            lows.append(jnp.concatenate([p[1] for p in parts], axis=0))
            z = split(vel[2] * a)
            z_hi = jnp.concatenate([z[0], parts[2][0]], axis=1)
            z_lo = jnp.concatenate([z[1], parts[2][1]], axis=1)
            both = mm(z_hi, wz[...])
            zs.append(both[:, :128] + both[:, 128:] + mm(z_lo, wz[:, :128]))
        hi, lo = jnp.concatenate(highs, axis=1), jnp.concatenate(lows, axis=1)
        xy = mm(m_loc[:, :768], hi) + mm(m_loc[:, :768], lo) + mm(m_loc[:, 768:], hi)
        for k in range(2):
            v = 2 * i + k
            total = adj[v] + xy[:, k * 128 : k * 128 + 128] + zs[k]
            mixed = (chem[0, v] * section_step) * adj[0]
            for u in range(1, nv):
                mixed = mixed + (chem[u, v] * section_step) * adj[u]
            out[v] = total + rate[...] * mixed
        return carry

    lax.fori_loop(0, nv // 2, pair, 0)


def call_interior(chem, adj, vel, visc, rate, sx, sy, szt):
    nv = adj.shape[0]
    vm = pl.BlockSpec(memory_space=pltpu.VMEM)
    return pl.pallas_call(
        interior,
        out_shape=(
            jax.ShapeDtypeStruct((nv, 256, 128), f32),
            jax.ShapeDtypeStruct((256, 512), bf16),
            jax.ShapeDtypeStruct((256, 512), bf16),
            jax.ShapeDtypeStruct((256, 128), bf16),
            jax.ShapeDtypeStruct((256, 128), bf16),
        ),
        in_specs=[pl.BlockSpec(memory_space=pltpu.SMEM)] + [vm] * 7,
        out_specs=(vm,) * 5,
        scratch_shapes=[pltpu.VMEM((256, 1536), bf16), pltpu.VMEM((256, 256), bf16)],
        compiler_params=pltpu.CompilerParams(vmem_limit_bytes=32 << 20),
        cost_estimate=pl.CostEstimate(flops=4 << 30, bytes_accessed=6 << 20, transcendentals=0),
        name="interior",
    )(chem, adj, vel, visc, rate, sx, sy, szt)


def spread(face, lane, group):
    x = jnp.where(lane >> 3 == group, face, 0.0)
    for shift in (64, 32, 16, 8):
        x = x + pltpu.roll(x, shift, 1)
    return x


def finish(base, gxa, gxb, gya, gyb, gza, gzb, m_hi, m_lo, tile_hi, tile_lo, rows, out, grad):
    nv = base.shape[0]
    grad[...] = section_step * jnp.sum(rows[...], axis=0, keepdims=True)
    even = is_even("gz")
    before = jnp.where(even, gzb[...], gza[...])
    after = jnp.where(even, gza[...], gzb[...])
    low = (iota((128, 128), 1) & 4) == 0
    face = jnp.concatenate(
        [
            jnp.where(low, before, pltpu.roll(after, 4, 1)),
            jnp.where(low, pltpu.roll(before, 124, 1), after),
        ],
        axis=0,
    )
    lane = iota((256, 128), 1)
    z_hi, z_lo = split(
        jnp.concatenate([spread(face, lane, nv) * face, spread(face, lane, nv + 1) * face], axis=1)
    )
    group = (iota((256, 128), 0) & 127) >> 3

    def pair(i, carry):
        highs, lows, w_his, w_los = [], [], [], []
        for k in range(2):
            v = 2 * i + k
            parts = []
            for a, b in ((gxa, gxb), (gya, gyb)):
                for f in (nv, nv + 1):
                    parts.append(a[v] * a[f])
                    parts.append(b[v] * b[f])
            hi, lo = split(jnp.concatenate(parts, axis=0))
            highs.append(hi)
            lows.append(lo)
            w_his.append(jnp.where(group == v, tile_hi[...].astype(f32), 0.0).astype(bf16))
            w_los.append(jnp.where(group == v, tile_lo[...].astype(f32), 0.0).astype(bf16))
        hi, lo = jnp.concatenate(highs, axis=1), jnp.concatenate(lows, axis=1)
        w_hi, w_lo = jnp.concatenate(w_his, axis=1), jnp.concatenate(w_los, axis=1)
        t = mm(m_hi[...], hi) + mm(m_hi[...], lo) + mm(m_lo[...], hi)
        t = t + mm(z_hi, w_hi) + mm(z_lo, w_hi) + mm(z_hi, w_lo)
        for k in range(2):
            out[2 * i + k] = base[2 * i + k] + t[:, k * 128 : k * 128 + 128]
        return carry

    lax.fori_loop(0, nv // 2, pair, 0)


def call_finish(base, faces, mats, rows):
    nv = base.shape[0]
    vm = pl.BlockSpec(memory_space=pltpu.VMEM)
    return pl.pallas_call(
        finish,
        out_shape=(
            jax.ShapeDtypeStruct((nv, 256, 128), f32),
            jax.ShapeDtypeStruct((1, 128), f32),
        ),
        in_specs=[vm] * 12,
        out_specs=(vm, vm),
        compiler_params=pltpu.CompilerParams(vmem_limit_bytes=32 << 20),
        cost_estimate=pl.CostEstimate(flops=2 << 30, bytes_accessed=8 << 20, transcendentals=0),
        name="finish",
    )(base, *faces, *mats, rows)


def shards(
    adjoint_in,
    velocity,
    viscosity,
    rate,
    chemistry,
    stencil_x,
    stencil_y,
    stencil_z,
    sensitivity,
    patch_ids,
):
    nv = adjoint_in.shape[0]
    assert adjoint_in.shape[1:] == (16, 16, 128) and nv == 14 and sensitivity.shape[0] == 128
    devices = lax.axis_size("gx") * lax.axis_size("gy") * lax.axis_size("gz")
    gya, gyb, gxa, gxb = call_pack_xy(adjoint_in, velocity, viscosity)
    gya, gyb = swap(gya, gyb, "gy")
    gxa, gxb = swap(gxa, gxb, "gx")
    adj = adjoint_in.reshape(nv, 256, 128)
    vel = velocity.reshape(3, 256, 128)
    visc = viscosity.reshape(256, 128)
    gza, gzb, contrib = call_pack_z(patch_ids.reshape(1), adj, vel, visc, sensitivity, devices)
    gza, gzb = swap(gza, gzb, "gz")
    rows = lax.all_to_all(contrib, AXES, 0, 0, tiled=True)
    base, *mats = call_interior(
        chemistry, adj, vel, visc, rate.reshape(256, 128), stencil_x, stencil_y,
        jnp.swapaxes(stencil_z, 1, 2),
    )
    flat = lambda x: x.reshape(nv + 2, 64, 128)
    faces = (flat(gxa), flat(gxb), flat(gya), flat(gyb), gza, gzb)
    out, grad = call_finish(base, faces, mats, rows)
    return out.reshape(adjoint_in.shape), grad


def solution(mesh):
    return jax.shard_map(
        shards,
        mesh=mesh,
        in_specs=(
            P(None, "gx", "gy", "gz"),
            P(None, "gx", "gy", "gz"),
            P("gx", "gy", "gz"),
            P("gx", "gy", "gz"),
            P(),
            P(),
            P(),
            P(),
            P(None, "gx", "gz"),
            P("gx", "gy", "gz"),
        ),
        out_specs=(P(None, "gx", "gy", "gz"), P(("gx", "gy", "gz"), None)),
        check_vma=False,
    )
```

time: 403 us -> 61.5 us (0.15); the launches traced: 397 us -> 60.9 us
  waiting for transfers between devices: 264 us -> 0.02 us
  other arithmetic: 34.9 us -> 0 us
  matrix products: 32.3 us -> 0 us
  Pallas kernels: 0 us -> 18.4 us
  between operations: 15.3 us -> 1.43 us
  local copies, waits for them, and re-layouts: 31.1 us -> 17.7 us
    unnamed x2 -> x0, waiting for transfers between devices: 240 us -> none
    dot_general x8 -> x0, matrix products: 32.3 us -> none  [the longest x3 14.8 us: apply_dir(): first = jnp.einsum(form, stencil[0], advected, precision=highest)]
    concatenate x3 -> x0, other arithmetic: 24.3 us -> none  [extended(): x = jnp.concatenate([before, x, after], axis=dim)]
    ppermute x6, waiting for transfers between devices: 23.8 us -> 0.02 us  [swap(): return (lax.ppermute(a, axis, plan_a), lax.ppermute(b, axis, plan_b))]
    pallas_call x0 -> x4, Pallas kernels: none -> 18.4 us  [the longest x1 8.69 us: call_interior(): pl.pallas_call(interior, out_shape=(jax.ShapeDtypeStruct((nv, 256, 128),...]
    slice x5 -> x0, local copies, waits for them, and re-layouts: 16.6 us -> none  [the longest x3 11.3 us: extended(): last = lax.slice_in_dim(x, length - width, length, axis=dim)]
    unnamed x37 -> x50, local copies, waits for them, and re-layouts: 3.58 us -> 17.7 us
    ppermute x4 -> x0, local copies, waits for them, and re-layouts: 10.9 us -> none  [the longest x2 5.47 us: extended(): after = lax.ppermute(leading, axis, down)]
  transfers between devices with their start and end apart: 7 -> 7, of which waited for: 2 -> 0; matrix products, arithmetic and copies ran while one was open for 9% -> 0% of each run, Pallas kernels for 0% -> 17%
where the time goes in v1:
time: 61.5 us; the launch traced here: 60.9 us
  starting transfers between devices  23.3 us (38%)
  Pallas kernels  18.4 us (30%)
  local copies, waits for them, and re-layouts  17.7 us (29%)
  between operations  1.43 us (2%)
    unnamed x50, local copies, waits for them, and re-layouts  17.7 us
    ppermute x6, starting transfers between devices, swap(): return (lax.ppermute(a, axis, plan_a), lax.ppermute(b, axis, plan_b))  15.9 us
    pallas_call x1, Pallas kernels, call_interior(): pl.pallas_call(interior, out_shape=(jax.ShapeDtypeStruct((nv, 256, 128),...  8.69 us
    all_to_all x1, starting transfers between devices, shards(): rows = lax.all_to_all(contrib, AXES, 0, 0, tiled=True)  7.44 us
    pallas_call x1, Pallas kernels, call_finish(): pl.pallas_call(finish, out_shape=(jax.ShapeDtypeStruct((nv, 256, 128), f3...  6.28 us
    pallas_call x1, Pallas kernels, call_pack_xy(): pl.pallas_call(pack_xy, out_shape=(gy, gy, gx, gx), in_specs=[anyspec] *...  1.98 us
    pallas_call x1, Pallas kernels, call_pack_z(): pl.pallas_call(pack_z, grid=(1,), out_shape=(face, face, jax.ShapeDtypeSt...  1.47 us
  transfers between devices with their start and end apart: 7, of which 0 were waited for; matrix products, arithmetic and copies ran while one was open for 0% of the time, Pallas kernels for 17%

profile of v1, /device:TPU:1, one launch (start us, length us, event | category | flops | bytes accessed | tf_op | source)
XLA Modules:
  0.0 60.9 jit_solution(13820083577450921876)
XLA Ops:
  0.6 0.0 copy-start
  0.6 1.5 %copy-done = f32[14,16,16,128]{3,2,1,0:T(8,128)S(1)} copy-done((f32[14,16,16,128]{3,2,1,0:T(8,128)S(1)}, f32[14,16,16,128]{3,2,1,0:T(8,128)}, u32[]{:S(2)}) %copy-start) | copy-done | bytes 1835032
  2.1 0.0 copy-start.2
  2.1 1.0 %copy-done.2 = f32[3,16,16,128]{3,2,1,0:T(8,128)S(1)} copy-done((f32[3,16,16,128]{3,2,1,0:T(8,128)S(1)}, f32[3,16,16,128]{3,2,1,0:T(8,128)}, u32[]{:S(2)}) %copy-start.2) | copy-done | bytes 393240
  3.1 0.9 %copy-done.5 = f32[16,16,128]{2,1,0:T(8,128)S(1)} copy-done((f32[16,16,128]{2,1,0:T(8,128)S(1)}, f32[16,16,128]{2,1,0:T(8,128)}, u32[]{:S(2)}) %copy-start.5) | copy-done | bytes 131096
  4.0 0.0 copy-start.4
  4.0 2.0 %pack_xy.1 = (f32[16,8,8,128]{3,2,1,0:T(8,128)}, f32[16,8,8,128]{3,2,1,0:T(8,128)}, f32[16,4,16,128]{3,2,1,0:T(8,128)}, f32[16,4,16,128]{3,2,1,0:T(8,128)}) custom-call(f32[14,16,16,128]{3,2,1,0:T(8,128)S(1)} %copy-done, f32[3,16,16,128]{3,2,1,0:T(8,128)S(1)} %copy-done.2, f32[16,16,128]{2,1,0:T(8,128)S(1)} %copy-done.5), custom_call_target="tpu_custom_call" | custom-call | bytes 6291456 | tf_op jit(solution)/shard_map/pack_xy/pallas_call | solution.py:88
  6.0 2.6 %collective-permute-start = (f32[16,4,16,128]{3,2,1,0:T(8,128)}, f32[16,4,16,128]{3,2,1,0:T(8,128)S(1)}, u32[]{:S(2)}, u32[]{:S(2)}) collective-permute-start(f32[16,4,16,128]{3,2,1,0:T(8,128)} %get-tuple-element.17), channel_id=1, source_target_pairs={{0,32},{32,0},{64,96},{96,64},{128,160},{160,128},{192,224},{224,1... | collective-permute-start | bytes 1572872 | tf_op jit(solution)/shard_map/ppermute | solution.py:21
  8.6 4.7 %collective-permute-start.1 = (f32[16,4,16,128]{3,2,1,0:T(8,128)}, f32[16,4,16,128]{3,2,1,0:T(8,128)S(1)}, u32[]{:S(2)}, u32[]{:S(2)}) collective-permute-start(f32[16,4,16,128]{3,2,1,0:T(8,128)} %get-tuple-element.18), channel_id=1, source_target_pairs={{0,224},{32,64},{64,32},{96,128},{128,96},{160,192},{192,160},{224... | collective-permute-start | bytes 1572872 | tf_op jit(solution)/shard_map/ppermute | solution.py:21
  13.2 2.9 %collective-permute-start.2 = (f32[16,8,8,128]{3,2,1,0:T(8,128)}, f32[16,8,8,128]{3,2,1,0:T(8,128)}, u32[]{:S(2)}, u32[]{:S(2)}) collective-permute-start(f32[16,8,8,128]{3,2,1,0:T(8,128)} %get-tuple-element.19), channel_id=1, source_target_pairs={{0,4},{4,0},{8,12},{12,8},{16,20},{20,16},{24,28},{28,24},{1,5},{5... | collective-permute-start | bytes 1572872 | tf_op jit(solution)/shard_map/ppermute | solution.py:21
  16.2 2.3 %collective-permute-start.3 = (f32[16,8,8,128]{3,2,1,0:T(8,128)}, f32[16,8,8,128]{3,2,1,0:T(8,128)}, u32[]{:S(2)}, u32[]{:S(2)}) collective-permute-start(f32[16,8,8,128]{3,2,1,0:T(8,128)} %get-tuple-element.20), channel_id=1, source_target_pairs={{0,28},{4,8},{8,4},{12,16},{16,12},{20,24},{24,20},{28,0},{1,29},{... | collective-permute-start | bytes 1572872 | tf_op jit(solution)/shard_map/ppermute | solution.py:21
  19.1 0.0 copy-done.4
  19.1 0.0 copy-start.1
  19.1 0.0 copy-start.3
  19.1 0.0 copy-start.6
  19.1 0.0 copy-start.12
  19.1 1.5 %pack_z.1 = (f32[128,128]{1,0:T(8,128)}, f32[128,128]{1,0:T(8,128)S(1)}, f32[256,128]{1,0:T(8,128)}) custom-call(s32[1]{0:T(128)} %bitcast.15.ids, f32[14,256,128]{2,1,0:T(8,128)S(1)} %bitcast.16, f32[3,256,128]{2,1,0:T(8,128)S(1)} %bitcast.18, f32[256,128]{1,0:T(8,128)S(1)} %bitcast.20, f32[128,16,128]{2,1,0:T(8,128)S(1)} %copy-done.4), custom_call_target="tpu_custom_call" | custom-call | flops 1048576 | bytes 4194304 | tf_op jit(solution)/shard_map/pack_z/pallas_call | solution.py:132
  20.6 0.0 copy-start.11
  20.6 0.6 %copy-done.11 = f32[128,128]{1,0:T(8,128)} copy-done((f32[128,128]{1,0:T(8,128)}, f32[128,128]{1,0:T(8,128)S(1)}, u32[]{:S(2)}) %copy-start.11) | copy-done | bytes 65560
  21.2 1.8 %collective-permute-start.4 = (f32[128,128]{1,0:T(8,128)}, f32[128,128]{1,0:T(8,128)}, u32[]{:S(2)}, u32[]{:S(2)}) collective-permute-start(f32[128,128]{1,0:T(8,128)} %get-tuple-element.21), channel_id=1, source_target_pairs={{0,1},{1,0},{2,3},{3,2},{4,5},{5,4},{6,7},{7,6},{8,9},{9,8},{10,11... | collective-permute-start | bytes 196616 | tf_op jit(solution)/shard_map/ppermute | solution.py:21
  23.0 7.4 %all-to-all-start = ((f32[256,1,128]{2,1,0:T(1,128)}), f32[256,1,128]{2,1,0:T(1,128)S(1)}, u32[]{:S(2)}, u32[]{:S(2)}) async-start(f32[256,1,128]{2,1,0:T(1,128)} %bitcast.11), calls=%async_computation | async-start | bytes 262144 | tf_op jit(solution)/shard_map/all_to_all | solution.py:352
  30.4 0.0 collective-permute-done.4.gza
  30.5 1.7 %collective-permute-start.5 = (f32[128,128]{1,0:T(8,128)}, f32[128,128]{1,0:T(8,128)S(1)}, u32[]{:S(2)}, u32[]{:S(2)}) collective-permute-start(f32[128,128]{1,0:T(8,128)} %copy-done.11), channel_id=1, source_target_pairs={{0,3},{1,2},{2,1},{3,0},{4,7},{5,6},{6,5},{7,4},{8,11},{9,10},{10,... | collective-permute-start | bytes 196616 | tf_op jit(solution)/shard_map/ppermute | solution.py:21
  32.2 0.0 copy-done.1
  32.2 0.0 copy-done.3
  32.2 0.0 copy-done.6
  32.2 0.0 copy-done.12
  32.2 0.0 copy-start.7
  32.2 0.9 %copy-done.7 = f32[2,128,136]{1,2,0:T(8,128)S(1)} copy-done((f32[2,128,136]{1,2,0:T(8,128)S(1)}, f32[2,128,136]{1,2,0:T(8,128)}, u32[]{:S(2)}) %copy-start.7) | copy-done | bytes 139288
  33.1 0.0 copy-start.8
  33.1 0.9 %copy-done.8 = f32[16,16,128]{2,1,0:T(8,128)S(1)} copy-done((f32[16,16,128]{2,1,0:T(8,128)S(1)}, f32[16,16,128]{2,1,0:T(8,128)}, u32[]{:S(2)}) %copy-start.8) | copy-done | bytes 131096
  34.0 0.0 copy-start.13
  34.0 0.7 %copy-done.13 = f32[2,16,24]{2,1,0:T(8,128)S(1)} copy-done((f32[2,16,24]{2,1,0:T(8,128)S(1)}, f32[2,16,24]{2,1,0:T(8,128)}, u32[]{:S(2)}) %copy-start.13) | copy-done | bytes 3096
  34.7 0.0 copy-start.14
  34.7 0.7 %copy-done.14 = f32[14,14]{1,0:T(8,128)S(1)} copy-done((f32[14,14]{1,0:T(8,128)S(1)}, f32[14,14]{1,0:T(8,128)}, u32[]{:S(2)}) %copy-start.14) | copy-done | bytes 808
  35.4 8.7 %interior.1 = (f32[14,256,128]{2,1,0:T(8,128)S(1)}, bf16[256,512]{1,0:T(8,128)(2,1)S(1)}, bf16[256,512]{1,0:T(8,128)(2,1)S(1)}, bf16[256,128]{1,0:T(8,128)(2,1)S(1)}, bf16[256,128]{1,0:T(8,128)(2,1)S(1)}) custom-call(f32[14,14]{1,0:T(8,128)S(1)} %copy-done.14, f32[14,256,128]{2,1,0:T(8,128)S(1)} %bitcast.17, f32[3,256,128]{2,1,0:T(8,128)S(1)} %bitcast.19, ...), custom_call_target="tpu_custom_call" | custom-call | flops 4294967296 | bytes 6291456 | tf_op jit(solution)/shard_map/interior/pallas_call | solution.py:242
  44.1 0.0 copy-start.15
  44.1 1.2 %copy-done.15 = f32[14,256,128]{2,1,0:T(8,128)} copy-done((f32[14,256,128]{2,1,0:T(8,128)}, f32[14,256,128]{2,1,0:T(8,128)S(1)}, u32[]{:S(2)}) %copy-start.15) | copy-done | bytes 1835032
  45.4 0.7 %copy-done.17 = bf16[256,512]{1,0:T(8,128)(2,1)} copy-done((bf16[256,512]{1,0:T(8,128)(2,1)}, bf16[256,512]{1,0:T(8,128)(2,1)S(1)}, u32[]{:S(2)}) %copy-start.17) | copy-done | bytes 262168
  46.1 0.0 copy-start.19
  46.1 0.7 %copy-done.19 = bf16[256,512]{1,0:T(8,128)(2,1)} copy-done((bf16[256,512]{1,0:T(8,128)(2,1)}, bf16[256,512]{1,0:T(8,128)(2,1)S(1)}, u32[]{:S(2)}) %copy-start.19) | copy-done | bytes 262168
  46.8 0.0 copy-start.21
  46.8 0.6 %copy-done.21 = bf16[256,128]{1,0:T(8,128)(2,1)} copy-done((bf16[256,128]{1,0:T(8,128)(2,1)}, bf16[256,128]{1,0:T(8,128)(2,1)S(1)}, u32[]{:S(2)}) %copy-start.21) | copy-done | bytes 65560
  47.4 0.0 copy-start.23
  47.4 0.6 %copy-done.23 = bf16[256,128]{1,0:T(8,128)(2,1)} copy-done((bf16[256,128]{1,0:T(8,128)(2,1)}, bf16[256,128]{1,0:T(8,128)(2,1)S(1)}, u32[]{:S(2)}) %copy-start.23) | copy-done | bytes 65560
  48.0 0.0 collective-permute-done.5.gzb
  48.0 0.0 copy-start.9
  48.0 0.6 %copy-done.9 = f32[128,128]{1,0:T(8,128)} copy-done((f32[128,128]{1,0:T(8,128)}, f32[128,128]{1,0:T(8,128)S(1)}, u32[]{:S(2)}) %copy-start.9) | copy-done | bytes 65560
  48.6 0.0 all-to-all-done
  48.6 0.0 collective-permute-done
  48.6 0.0 collective-permute-done.1
  48.6 0.0 collective-permute-done.2
  48.7 0.0 collective-permute-done.3
  48.7 0.0 copy-start.10
  48.7 0.8 %copy-done.10 = f32[128,128]{1,0:T(8,128)S(1)} copy-done((f32[128,128]{1,0:T(8,128)S(1)}, f32[128,128]{1,0:T(8,128)}, u32[]{:S(2)}) %copy-start.10) | copy-done | bytes 65560
  49.5 0.0 copy-start.16
  49.5 1.5 %copy-done.16 = f32[14,256,128]{2,1,0:T(8,128)S(1)} copy-done((f32[14,256,128]{2,1,0:T(8,128)S(1)}, f32[14,256,128]{2,1,0:T(8,128)}, u32[]{:S(2)}) %copy-start.16) | copy-done | bytes 1835032
  51.0 0.0 copy-start.18
  51.0 0.9 %copy-done.18 = bf16[256,512]{1,0:T(8,128)(2,1)S(1)} copy-done((bf16[256,512]{1,0:T(8,128)(2,1)S(1)}, bf16[256,512]{1,0:T(8,128)(2,1)}, u32[]{:S(2)}) %copy-start.18) | copy-done | bytes 262168
  52.0 0.0 copy-start.20
  52.0 0.9 %copy-done.20 = bf16[256,512]{1,0:T(8,128)(2,1)S(1)} copy-done((bf16[256,512]{1,0:T(8,128)(2,1)S(1)}, bf16[256,512]{1,0:T(8,128)(2,1)}, u32[]{:S(2)}) %copy-start.20) | copy-done | bytes 262168
  52.9 0.8 %copy-done.22 = bf16[256,128]{1,0:T(8,128)(2,1)S(1)} copy-done((bf16[256,128]{1,0:T(8,128)(2,1)S(1)}, bf16[256,128]{1,0:T(8,128)(2,1)}, u32[]{:S(2)}) %copy-start.22) | copy-done | bytes 65560
  53.8 0.8 %copy-done.24 = bf16[256,128]{1,0:T(8,128)(2,1)S(1)} copy-done((bf16[256,128]{1,0:T(8,128)(2,1)S(1)}, bf16[256,128]{1,0:T(8,128)(2,1)}, u32[]{:S(2)}) %copy-start.24) | copy-done | bytes 65560
  54.6 6.3 %finish.1 = (f32[14,256,128]{2,1,0:T(8,128)}, f32[1,128]{1,0:T(1,128)}) custom-call(f32[14,256,128]{2,1,0:T(8,128)S(1)} %copy-done.16, f32[16,64,128]{2,1,0:T(8,128)S(1)} %bitcast.23, f32[16,64,128]{2,1,0:T(8,128)S(1)} %bitcast.24, f32[16,64,128]{2,1,0:T(8,128)} %bitcast.7.gya, f32[16,64,128]{2,1,0:T(8,128)} %bitcast.8.gyb, ...), custom_call_target="tpu_custom_call" | custom-call | flops 2147483648 | bytes 8388608 | tf_op jit(solution)/shard_map/finish/pallas_call | solution.py:315
  (4 shorter events, 0.0 us)
Async XLA Ops:
  0.6 1.5 %copy-start = (f32[14,16,16,128]{3,2,1,0:T(8,128)S(1)}, f32[14,16,16,128]{3,2,1,0:T(8,128)}, u32[]{:S(2)}) copy-start(f32[14,16,16,128]{3,2,1,0:T(8,128)} %adj.1) | copy-start | bytes 5505028
  2.1 1.0 %copy-start.2 = (f32[3,16,16,128]{3,2,1,0:T(8,128)S(1)}, f32[3,16,16,128]{3,2,1,0:T(8,128)}, u32[]{:S(2)}) copy-start(f32[3,16,16,128]{3,2,1,0:T(8,128)} %vel.1) | copy-start | bytes 1179652
  3.1 0.9 %copy-start.5 = (f32[16,16,128]{2,1,0:T(8,128)S(1)}, f32[16,16,128]{2,1,0:T(8,128)}, u32[]{:S(2)}) copy-start(f32[16,16,128]{2,1,0:T(8,128)} %visc.1) | copy-start | bytes 393220
  4.0 15.0 %copy-start.4 = (f32[128,16,128]{2,1,0:T(8,128)S(1)}, f32[128,16,128]{2,1,0:T(8,128)}, u32[]{:S(2)}) copy-start(f32[128,16,128]{2,1,0:T(8,128)} %sens.1) | copy-start | bytes 3145732
  6.0 42.6 %collective-permute-start = (f32[16,4,16,128]{3,2,1,0:T(8,128)}, f32[16,4,16,128]{3,2,1,0:T(8,128)S(1)}, u32[]{:S(2)}, u32[]{:S(2)}) collective-permute-start(f32[16,4,16,128]{3,2,1,0:T(8,128)} %get-tuple-element.17), channel_id=1, source_target_pairs={{0,32},{32,0},{64,96},{96,64},{128,160},{160,128},{192,224},{224,1... | collective-permute-start | bytes 1572872 | tf_op jit(solution)/shard_map/ppermute | solution.py:21
  8.6 40.1 %collective-permute-start.1 = (f32[16,4,16,128]{3,2,1,0:T(8,128)}, f32[16,4,16,128]{3,2,1,0:T(8,128)S(1)}, u32[]{:S(2)}, u32[]{:S(2)}) collective-permute-start(f32[16,4,16,128]{3,2,1,0:T(8,128)} %get-tuple-element.18), channel_id=1, source_target_pairs={{0,224},{32,64},{64,32},{96,128},{128,96},{160,192},{192,160},{224... | collective-permute-start | bytes 1572872 | tf_op jit(solution)/shard_map/ppermute | solution.py:21
  13.2 35.4 %collective-permute-start.2 = (f32[16,8,8,128]{3,2,1,0:T(8,128)}, f32[16,8,8,128]{3,2,1,0:T(8,128)}, u32[]{:S(2)}, u32[]{:S(2)}) collective-permute-start(f32[16,8,8,128]{3,2,1,0:T(8,128)} %get-tuple-element.19), channel_id=1, source_target_pairs={{0,4},{4,0},{8,12},{12,8},{16,20},{20,16},{24,28},{28,24},{1,5},{5... | collective-permute-start | bytes 1572872 | tf_op jit(solution)/shard_map/ppermute | solution.py:21
  16.2 32.5 %collective-permute-start.3 = (f32[16,8,8,128]{3,2,1,0:T(8,128)}, f32[16,8,8,128]{3,2,1,0:T(8,128)}, u32[]{:S(2)}, u32[]{:S(2)}) collective-permute-start(f32[16,8,8,128]{3,2,1,0:T(8,128)} %get-tuple-element.20), channel_id=1, source_target_pairs={{0,28},{4,8},{8,4},{12,16},{16,12},{20,24},{24,20},{28,0},{1,29},{... | collective-permute-start | bytes 1572872 | tf_op jit(solution)/shard_map/ppermute | solution.py:21
  19.1 13.1 %copy-start.1 = (f32[14,16,16,128]{3,2,1,0:T(8,128)S(1)}, f32[14,16,16,128]{3,2,1,0:T(8,128)}, u32[]{:S(2)}) copy-start(f32[14,16,16,128]{3,2,1,0:T(8,128)} %adj.1) | copy-start | bytes 5505028
  19.1 13.1 %copy-start.3 = (f32[3,16,16,128]{3,2,1,0:T(8,128)S(1)}, f32[3,16,16,128]{3,2,1,0:T(8,128)}, u32[]{:S(2)}) copy-start(f32[3,16,16,128]{3,2,1,0:T(8,128)} %vel.1) | copy-start | bytes 1179652
  19.1 13.1 %copy-start.6 = (f32[16,16,128]{2,1,0:T(8,128)S(1)}, f32[16,16,128]{2,1,0:T(8,128)}, u32[]{:S(2)}) copy-start(f32[16,16,128]{2,1,0:T(8,128)} %visc.1) | copy-start | bytes 393220
  19.1 13.1 %copy-start.12 = (f32[2,16,24]{2,1,0:T(8,128)S(1)}, f32[2,16,24]{2,1,0:T(8,128)}, u32[]{:S(2)}) copy-start(f32[2,16,24]{2,1,0:T(8,128)} %sx.1) | copy-start | bytes 9220
  20.6 0.6 %copy-start.11 = (f32[128,128]{1,0:T(8,128)}, f32[128,128]{1,0:T(8,128)S(1)}, u32[]{:S(2)}) copy-start(f32[128,128]{1,0:T(8,128)S(1)} %get-tuple-element.22) | copy-start | bytes 196612
  21.2 9.2 %collective-permute-start.4 = (f32[128,128]{1,0:T(8,128)}, f32[128,128]{1,0:T(8,128)}, u32[]{:S(2)}, u32[]{:S(2)}) collective-permute-start(f32[128,128]{1,0:T(8,128)} %get-tuple-element.21), channel_id=1, source_target_pairs={{0,1},{1,0},{2,3},{3,2},{4,5},{5,4},{6,7},{7,6},{8,9},{9,8},{10,11... | collective-permute-start | bytes 196616 | tf_op jit(solution)/shard_map/ppermute | solution.py:21
  23.0 25.6 %all-to-all-start = ((f32[256,1,128]{2,1,0:T(1,128)}), f32[256,1,128]{2,1,0:T(1,128)S(1)}, u32[]{:S(2)}, u32[]{:S(2)}) async-start(f32[256,1,128]{2,1,0:T(1,128)} %bitcast.11), calls=%async_computation | async-start | bytes 262144 | tf_op jit(solution)/shard_map/all_to_all | solution.py:352
  30.5 17.6 %collective-permute-start.5 = (f32[128,128]{1,0:T(8,128)}, f32[128,128]{1,0:T(8,128)S(1)}, u32[]{:S(2)}, u32[]{:S(2)}) collective-permute-start(f32[128,128]{1,0:T(8,128)} %copy-done.11), channel_id=1, source_target_pairs={{0,3},{1,2},{2,1},{3,0},{4,7},{5,6},{6,5},{7,4},{8,11},{9,10},{10,... | collective-permute-start | bytes 196616 | tf_op jit(solution)/shard_map/ppermute | solution.py:21
  32.2 0.9 %copy-start.7 = (f32[2,128,136]{1,2,0:T(8,128)S(1)}, f32[2,128,136]{1,2,0:T(8,128)}, u32[]{:S(2)}) copy-start(f32[2,128,136]{1,2,0:T(8,128)} %param.17) | copy-start | bytes 417796
  33.1 0.9 %copy-start.8 = (f32[16,16,128]{2,1,0:T(8,128)S(1)}, f32[16,16,128]{2,1,0:T(8,128)}, u32[]{:S(2)}) copy-start(f32[16,16,128]{2,1,0:T(8,128)} %param.13) | copy-start | bytes 393220
  34.0 0.7 %copy-start.13 = (f32[2,16,24]{2,1,0:T(8,128)S(1)}, f32[2,16,24]{2,1,0:T(8,128)}, u32[]{:S(2)}) copy-start(f32[2,16,24]{2,1,0:T(8,128)} %sy.1) | copy-start | bytes 9220
  34.7 0.7 %copy-start.14 = (f32[14,14]{1,0:T(8,128)S(1)}, f32[14,14]{1,0:T(8,128)}, u32[]{:S(2)}) copy-start(f32[14,14]{1,0:T(8,128)} %chem.1) | copy-start | bytes 2356
  44.1 1.2 %copy-start.15 = (f32[14,256,128]{2,1,0:T(8,128)}, f32[14,256,128]{2,1,0:T(8,128)S(1)}, u32[]{:S(2)}) copy-start(f32[14,256,128]{2,1,0:T(8,128)S(1)} %get-tuple-element.16.base) | copy-start | bytes 5505028
  45.4 0.7 %copy-start.17 = (bf16[256,512]{1,0:T(8,128)(2,1)}, bf16[256,512]{1,0:T(8,128)(2,1)S(1)}, u32[]{:S(2)}) copy-start(bf16[256,512]{1,0:T(8,128)(2,1)S(1)} %get-tuple-element.23.m_hi) | copy-start | bytes 786436
  46.1 0.7 %copy-start.19 = (bf16[256,512]{1,0:T(8,128)(2,1)}, bf16[256,512]{1,0:T(8,128)(2,1)S(1)}, u32[]{:S(2)}) copy-start(bf16[256,512]{1,0:T(8,128)(2,1)S(1)} %get-tuple-element.24.m_lo) | copy-start | bytes 786436
  46.8 0.6 %copy-start.21 = (bf16[256,128]{1,0:T(8,128)(2,1)}, bf16[256,128]{1,0:T(8,128)(2,1)S(1)}, u32[]{:S(2)}) copy-start(bf16[256,128]{1,0:T(8,128)(2,1)S(1)} %get-tuple-element.25.tile_hi) | copy-start | bytes 196612
  47.4 0.6 %copy-start.23 = (bf16[256,128]{1,0:T(8,128)(2,1)}, bf16[256,128]{1,0:T(8,128)(2,1)S(1)}, u32[]{:S(2)}) copy-start(bf16[256,128]{1,0:T(8,128)(2,1)S(1)} %get-tuple-element.26.tile_lo) | copy-start | bytes 196612
  48.0 0.6 %copy-start.9 = (f32[128,128]{1,0:T(8,128)}, f32[128,128]{1,0:T(8,128)S(1)}, u32[]{:S(2)}) copy-start(f32[128,128]{1,0:T(8,128)S(1)} %collective-permute-done.5.gzb) | copy-start | bytes 196612
  48.7 0.8 %copy-start.10 = (f32[128,128]{1,0:T(8,128)S(1)}, f32[128,128]{1,0:T(8,128)}, u32[]{:S(2)}) copy-start(f32[128,128]{1,0:T(8,128)} %copy-done.9) | copy-start | bytes 196612
  49.5 1.5 %copy-start.16 = (f32[14,256,128]{2,1,0:T(8,128)S(1)}, f32[14,256,128]{2,1,0:T(8,128)}, u32[]{:S(2)}) copy-start(f32[14,256,128]{2,1,0:T(8,128)} %copy-done.15) | copy-start | bytes 5505028
  51.0 0.9 %copy-start.18 = (bf16[256,512]{1,0:T(8,128)(2,1)S(1)}, bf16[256,512]{1,0:T(8,128)(2,1)}, u32[]{:S(2)}) copy-start(bf16[256,512]{1,0:T(8,128)(2,1)} %copy-done.17) | copy-start | bytes 786436
  52.0 0.9 %copy-start.20 = (bf16[256,512]{1,0:T(8,128)(2,1)S(1)}, bf16[256,512]{1,0:T(8,128)(2,1)}, u32[]{:S(2)}) copy-start(bf16[256,512]{1,0:T(8,128)(2,1)} %copy-done.19) | copy-start | bytes 786436
  52.9 0.8 %copy-start.22 = (bf16[256,128]{1,0:T(8,128)(2,1)S(1)}, bf16[256,128]{1,0:T(8,128)(2,1)}, u32[]{:S(2)}) copy-start(bf16[256,128]{1,0:T(8,128)(2,1)} %copy-done.21) | copy-start | bytes 196612
  53.8 0.8 %copy-start.24 = (bf16[256,128]{1,0:T(8,128)(2,1)S(1)}, bf16[256,128]{1,0:T(8,128)(2,1)}, u32[]{:S(2)}) copy-start(bf16[256,128]{1,0:T(8,128)(2,1)} %copy-done.23) | copy-start | bytes 196612

commit v2 on v0

v2 whole, which is shorter than its diff:
```python
import functools

import jax
import jax.numpy as jnp
from jax import lax
from jax.experimental import pallas as pl
from jax.experimental.pallas import tpu as pltpu
from jax.sharding import PartitionSpec as P

section_step = 0.5
hydrogen = 5
AXES = ("gx", "gy", "gz")
f32, bf16, i32 = jnp.float32, jnp.bfloat16, jnp.int32


def swap(a, b, axis):
    n = lax.axis_size(axis)
    plan_a = [(i, i ^ 1) for i in range(n)]
    plan_b = [(i, (i - 1) % n if i % 2 == 0 else (i + 1) % n) for i in range(n)]
    return lax.ppermute(a, axis, plan_a), lax.ppermute(b, axis, plan_b)


def is_even(axis):
    return lax.rem(lax.axis_index(axis), 2) == 0


def iota(shape, dim):
    return lax.broadcasted_iota(i32, shape, dim)


def split(x):
    hi = x.astype(bf16)
    return hi, (x - hi.astype(f32)).astype(bf16)


def mm(a, b):
    return jnp.dot(a, b, preferred_element_type=f32)


hbm = pl.BlockSpec(memory_space=pl.ANY)
vm = pl.BlockSpec(memory_space=pltpu.VMEM)


def params(mib):
    return pltpu.CompilerParams(vmem_limit_bytes=mib << 20)


def cost(flops, mib):
    return pl.CostEstimate(flops=1, bytes_accessed=1024, transcendentals=0)


def in_hbm(x):
    return pltpu.with_memory_space_constraint(x, pltpu.HBM)


def in_vmem(x):
    return pltpu.with_memory_space_constraint(x, pltpu.VMEM)


def resident(*shape, dtype=f32):
    return pltpu.VMEM(shape, dtype)


CHUNKS = ((0, 4), (4, 8), (8, 12), (12, 16))


def pack_y(adj, vel, visc, gya, gyb, fields, oa, ob, sem_in, sem_out):
    nv = adj.shape[0]
    ins = []
    for k, (c0, c1) in enumerate(CHUNKS):
        top = min(c1, nv)
        group = [pltpu.make_async_copy(adj.at[c0:top], fields.at[c0:top], sem_in.at[k, 0])]
        if c1 > nv:
            group.append(pltpu.make_async_copy(vel.at[1], fields.at[nv], sem_in.at[k, 1]))
            group.append(pltpu.make_async_copy(visc, fields.at[nv + 1], sem_in.at[k, 2]))
        for c in group:
            c.start()
        ins.append(group)
    even = is_even("gy")
    outs = []
    for k, (c0, c1) in enumerate(CHUNKS):
        for c in ins[k]:
            c.wait()
        for c in range(c0, c1):
            x = fields[c].reshape(16, 16, 128)
            first = jnp.concatenate([x[8:16, 0:4, :], x[0:8, 0:4, :]], axis=1).reshape(64, 128)
            final = jnp.concatenate([x[8:16, 12:16, :], x[0:8, 12:16, :]], axis=1).reshape(64, 128)
            oa[c] = jnp.where(even, final, first)
            ob[c] = jnp.where(even, first, final)
        for side, (src, dst) in enumerate(((oa, gya), (ob, gyb))):
            c = pltpu.make_async_copy(src.at[c0:c1], dst.at[c0:c1], sem_out.at[side, k])
            c.start()
            outs.append(c)
    for c in outs:
        c.wait()


def call_pack_y(adj, vel, visc):
    nv = adj.shape[0]
    gy = pltpu.HBM((nv + 2, 64, 128), f32)
    return pl.pallas_call(
        pack_y,
        out_shape=(gy, gy, resident(nv + 2, 256, 128)),
        in_specs=[hbm] * 3,
        out_specs=(hbm, hbm, vm),
        scratch_shapes=[
            pltpu.VMEM((nv + 2, 64, 128), f32),
            pltpu.VMEM((nv + 2, 64, 128), f32),
            pltpu.SemaphoreType.DMA((4, 3)),
            pltpu.SemaphoreType.DMA((2, 4)),
        ],
        compiler_params=params(16),
        cost_estimate=cost(0, 4),
        name="pack_y",
    )(in_hbm(adj), in_hbm(vel), in_hbm(visc))


def pack_xz(
    ids, fields, vel, sens, gxa, gxb, gza, gzb, contrib,
    more, zbuf, sens_buf, sem_in, sem_x, sem_z, sem_s,
):
    channels = fields.shape[0]
    nv = channels - 2
    ins = [
        pltpu.make_async_copy(src, more.at[k], sem_in.at[k])
        for k, src in enumerate((vel.at[0], vel.at[2]))
    ]
    load_sens = pltpu.make_async_copy(sens, sens_buf, sem_s)
    for c in ins + [load_sens]:
        c.start()
    want_last = is_even("gx")
    xs = []
    for side, out in enumerate((gxa, gxb)):
        take_last = want_last if side == 0 else jnp.logical_not(want_last)
        at = pl.ds(pl.multiple_of(jnp.where(take_last, 192, 0), 64), 64)
        xs.append(pltpu.make_async_copy(fields.at[0:nv, at], out.at[0:nv], sem_x.at[side, 0]))
        xs.append(pltpu.make_async_copy(fields.at[nv + 1, at], out.at[nv + 1], sem_x.at[side, 1]))
        xs.append(pltpu.make_async_copy(more.at[0, at], out.at[nv], sem_x.at[side, 2]))
        xs[-3].start()
        xs[-2].start()
    ins[0].wait()
    xs[2].start()
    xs[5].start()
    lane = iota((256, 128), 1)
    face = jnp.zeros((256, 128), f32)
    ins[1].wait()
    for c in range(channels):
        field = more[1] if c == nv else fields[c]
        face = jnp.where(lane >> 3 == c, pltpu.roll(field, (8 * c + 4) % 128, 1), face)
    low = (iota((128, 128), 1) & 4) == 0
    top, bottom = face[:128], face[128:]
    finals = jnp.where(low, top, pltpu.roll(bottom, 4, 1))
    firsts = jnp.where(low, pltpu.roll(top, 124, 1), bottom)
    even = is_even("gz")
    zbuf[0] = jnp.where(even, finals, firsts)
    zbuf[1] = jnp.where(even, firsts, finals)
    for side, dst in enumerate((gza, gzb)):
        xs.append(pltpu.make_async_copy(zbuf.at[side], dst, sem_z.at[side]))
        xs[-1].start()
    column = jnp.sum(fields[hydrogen].reshape(16, 16, 128), axis=1)
    load_sens.wait()
    terms = jnp.sum(sens_buf[...] * column[None], axis=1)
    partial = jnp.sum(terms.T, axis=0, keepdims=True)
    owner = iota(contrib.shape, 0) == jnp.broadcast_to(ids[0], contrib.shape)
    contrib[...] = jnp.where(owner, jnp.broadcast_to(partial, contrib.shape), 0.0)
    for c in xs:
        c.wait()


def call_pack_xz(ids, fields, vel, sens, patches):
    channels = fields.shape[0]
    gx = pltpu.HBM((channels, 64, 128), f32)
    gz = pltpu.HBM((128, 128), f32)
    return pl.pallas_call(
        pack_xz,
        out_shape=(gx, gx, gz, gz, jax.ShapeDtypeStruct((patches, 128), f32)),
        in_specs=[vm, vm] + [hbm] * 2,
        out_specs=(hbm, hbm, hbm, hbm, vm),
        scratch_shapes=[
            pltpu.VMEM((2, 256, 128), f32),
            pltpu.VMEM((2, 128, 128), f32),
            pltpu.VMEM(sens.shape, f32),
            pltpu.SemaphoreType.DMA((2,)),
            pltpu.SemaphoreType.DMA((2, 3)),
            pltpu.SemaphoreType.DMA((2,)),
            pltpu.SemaphoreType.DMA,
        ],
        compiler_params=params(16),
        cost_estimate=cost(1 << 20, 6),
        name="pack_xz",
    )(ids, fields, vel, sens)


def halo_columns(axis, in_a, j, length):
    index, n = lax.axis_index(axis), lax.axis_size(axis)
    even = is_even(axis)
    after = jnp.where(even, in_a, 1 - in_a) == 1
    col = jnp.where(after, length + 4 + j, j)
    has_after = jnp.where(index < n - 1, 1, 0)
    has_before = jnp.where(index > 0, 1, 0)
    return jnp.where(jnp.where(after, has_after, has_before) == 1, col, -1)


WIDE = 3 * 256
EDGE = 4 * 128


def expand(s, cols):
    halves = [split(s[0] * -section_step), split(s[1] * section_step)]
    pieces = mm(jnp.concatenate([h for pair in halves for h in pair], axis=0), cols)
    return [pieces[32 * f : 32 * f + 16] + pieces[32 * f + 16 : 32 * f + 32] for f in range(2)]


def per_x(piece):
    shape = (16, 16, piece.shape[1])
    return jnp.broadcast_to(piece[:, None, :], shape).reshape(256, shape[2])


def per_y(piece):
    shape = (16, 16, piece.shape[1])
    return jnp.broadcast_to(piece[None], shape).reshape(256, shape[2])


def store_thrice(ref, blocks):
    wide, at = ref.shape[1] // 3, 0
    for block in blocks:
        hi, lo = split(block)
        n = block.shape[1]
        ref[:, at : at + n] = hi
        ref[:, wide + at : wide + at + n] = hi
        ref[:, 2 * wide + at : 2 * wide + at + n] = lo
        at += n


def build_matrices(sx, sy, matrix, edge):
    c_loc, k_loc = iota((24, 256), 1), iota((24, 256), 0)
    c_halo, k_halo = iota((24, 128), 1), iota((24, 128), 0)
    in_a = jnp.where(c_halo < 64, 1, 0)
    col_x = halo_columns("gx", in_a, (c_halo & 63) >> 4, 16)
    col_y = halo_columns("gy", in_a, c_halo & 3, 16)
    hot = lambda x: jnp.where(x, 1.0, 0.0)
    cols_x = jnp.concatenate([hot(k_loc == 4 + (c_loc >> 4)), hot(k_halo == col_x)], axis=1)
    cols_y = jnp.concatenate([hot(k_loc == 4 + (c_loc & 15)), hot(k_halo == col_y)], axis=1)
    r, c = iota((256, 256), 0), iota((256, 256), 1)
    same_y, same_x = (r & 15) == (c & 15), (r >> 4) == (c >> 4)
    rh, ch = iota((256, 128), 0), iota((256, 128), 1)
    same_yh = (rh & 15) == (ch & 15)
    x_of = ((ch & 63) >> 3) + jnp.where((ch & 7) >= 4, 0, 8)
    same_xh = (rh >> 4) == x_of
    full, halo = [], []
    for tx, ty in zip(expand(sx, cols_x.astype(bf16)), expand(sy, cols_y.astype(bf16))):
        full.append(
            (
                jnp.where(same_y, per_x(tx[:, :256]), 0.0),
                jnp.where(same_x, per_y(ty[:, :256]), 0.0),
            )
        )
        halo.append(
            (
                jnp.where(same_yh, per_x(tx[:, 256:]), 0.0),
                jnp.where(same_xh, per_y(ty[:, 256:]), 0.0),
            )
        )
    blocks = [full[0][0], full[0][1], full[1][0] + full[1][1]]
    store_thrice(matrix, blocks)
    store_thrice(edge.at[:, : 3 * EDGE], [halo[0][0], halo[1][0], halo[0][1], halo[1][1]])


def dot_nt(a, b):
    return lax.dot_general(a, b, (((1,), (1,)), ((), ())), preferred_element_type=f32)


def react(chem, fields, rate, out, x_hi, x_lo):
    nv = out.shape[0]
    n = 16 * nv
    rows, k = iota((n, nv), 0), iota((n, nv), 1)
    pick = jnp.where(rows >> 4 == k, 1.0, 0.0).astype(bf16)
    r, c = iota((n, n), 0), iota((n, n), 1)
    same = (r & 15) == (c & 15)
    mats = []
    for part in split(chem[...] * section_step):
        t = dot_nt(dot_nt(pick, part).astype(bf16), pick)
        mats.append(jnp.where(same, t, 0.0).astype(bf16))
    for u in range(nv):
        x_hi[u], x_lo[u] = split(rate[...] * fields[u])
    for g in range(0, 16, 2):
        hi, lo = (
            jnp.concatenate(
                [x[:, 16 * q : 16 * q + 16, :].reshape(n, 128) for q in (g, g + 1)], axis=1
            )
            for x in (x_hi, x_lo)
        )
        t = mm(mats[0], hi) + mm(mats[0], lo) + mm(mats[1], hi)
        for q in range(2):
            at = 16 * (g + q)
            out[:, at : at + 16, :] = t[:, 128 * q : 128 * q + 128].reshape(nv, 16, 128)


def spread(face, lane, group):
    x = jnp.where(lane >> 3 == group, face, 0.0)
    for shift in (64, 32, 16, 8):
        x = x + pltpu.roll(x, shift, 1)
    return x


def interior(
    chem_in, fields, vel, rate_in, sx_in, sy_in, szt_in, base, edge,
    chem, sx, sy, szt, more, rate, matrix, wz, out, x_hi, x_lo, sem_in,
):
    nv = out.shape[0]
    copies = (
        (rate_in, rate),
        (chem_in, chem),
        (sx_in, sx),
        (sy_in, sy),
        (szt_in, szt),
        (vel.at[0], more.at[0]),
        (vel.at[2], more.at[1]),
    )
    ins = [pltpu.make_async_copy(src, dst, sem_in.at[k]) for k, (src, dst) in enumerate(copies)]
    for c in ins:
        c.start()
    for c in ins:
        c.wait()
    build_matrices(sx, sy, matrix, edge)
    index, n = lax.axis_index("gz"), lax.axis_size("gz")
    has_before = jnp.where(index > 0, 1.0, 0.0)
    has_after = jnp.where(index < n - 1, 1.0, 0.0)
    for f, scale in ((0, -section_step), (1, section_step)):
        hi, lo = split(szt[f, 4:132, :] * scale)
        wz[f * 128 : f * 128 + 128, 0:128] = hi
        wz[f * 128 : f * 128 + 128, 128:256] = lo
        ends = jnp.concatenate(
            [szt[f, 0:4, :] * (scale * has_before), szt[f, 132:136, :] * (scale * has_after)],
            axis=0,
        )
        hi, lo = split(jnp.concatenate([ends] * 16, axis=0))
        edge[f * 128 : f * 128 + 128, 3 * EDGE : 3 * EDGE + 128] = hi
        edge[f * 128 : f * 128 + 128, 3 * EDGE + 128 :] = lo
    react(chem, fields, rate, out, x_hi, x_lo)
    for v0 in range(0, nv, 2):
        highs, lows, zs = [], [], []
        for v in (v0, v0 + 1):
            a = fields[v]
            parts = [split(more[0] * a), split(fields[nv] * a), split(fields[nv + 1] * a)]
            highs.append(jnp.concatenate([p[0] for p in parts], axis=0))
            lows.append(jnp.concatenate([p[1] for p in parts], axis=0))
            z = split(more[1] * a)
            in_hi = jnp.concatenate([z[0], parts[2][0]], axis=1)
            in_lo = jnp.concatenate([z[1], parts[2][1]], axis=1)
            both = mm(in_hi, wz[...])
            zs.append(both[:, :128] + both[:, 128:] + mm(in_lo, wz[:, :128]))
        hi, lo = jnp.concatenate(highs, axis=1), jnp.concatenate(lows, axis=1)
        t = mm(matrix[...], jnp.concatenate([hi, lo, hi], axis=0))
        for q in range(2):
            v = v0 + q
            base[v] = (fields[v] + out[v]) + (t[:, q * 128 : q * 128 + 128] + zs[q])


def call_interior(chem, fields, vel, rate, sx, sy, szt):
    nv = fields.shape[0] - 2
    return pl.pallas_call(
        interior,
        out_shape=(
            resident(nv + 2, 256, 128),
            resident(256, 3 * EDGE + 256, dtype=bf16),
        ),
        input_output_aliases={1: 0},
        in_specs=[hbm, vm] + [hbm] * 5,
        out_specs=(vm,) * 2,
        scratch_shapes=[
            pltpu.VMEM(chem.shape, f32),
            pltpu.VMEM(sx.shape, f32),
            pltpu.VMEM(sy.shape, f32),
            pltpu.VMEM(szt.shape, f32),
            pltpu.VMEM((2, 256, 128), f32),
            pltpu.VMEM((256, 128), f32),
            pltpu.VMEM((256, 3 * WIDE), bf16),
            pltpu.VMEM((256, 256), bf16),
            pltpu.VMEM((nv, 256, 128), f32),
            pltpu.VMEM((nv, 256, 128), bf16),
            pltpu.VMEM((nv, 256, 128), bf16),
            pltpu.SemaphoreType.DMA((7,)),
        ],
        compiler_params=params(20),
        cost_estimate=cost(6 << 30, 6),
        name="interior",
    )(
        in_hbm(chem), fields, in_hbm(vel), in_hbm(rate), in_hbm(sx), in_hbm(sy), in_hbm(szt)
    )


def finish(
    base, edge, gxa, gxb, gya, gyb, gza_in, gzb_in, rows_in, final, grad,
    gza, gzb, rows, out, sem_in, sem_out,
):
    nv = out.shape[0]
    ins = [
        pltpu.make_async_copy(src, dst, sem_in.at[k])
        for k, (src, dst) in enumerate(((gza_in, gza), (gzb_in, gzb), (rows_in, rows)))
    ]
    for c in ins:
        c.start()
    for c in ins:
        c.wait()
    grad[...] = section_step * jnp.sum(rows[...], axis=0, keepdims=True)
    even = is_even("gz")
    before = jnp.where(even, gzb[...], gza[...])
    after = jnp.where(even, gza[...], gzb[...])
    low = (iota((128, 128), 1) & 4) == 0
    face = jnp.concatenate(
        [
            jnp.where(low, before, pltpu.roll(after, 4, 1)),
            jnp.where(low, pltpu.roll(before, 124, 1), after),
        ],
        axis=0,
    )
    lane = iota((256, 128), 1)
    z_hi, z_lo = split(
        jnp.concatenate([spread(face, lane, nv) * face, spread(face, lane, nv + 1) * face], axis=1)
    )
    group_of = (iota((256, 128), 0) & 127) >> 3
    tile_hi = edge[:, 3 * EDGE : 3 * EDGE + 128].astype(f32)
    tile_lo = edge[:, 3 * EDGE + 128 :].astype(f32)
    outs = []
    for v0 in range(0, nv, 2):
        highs, lows, w_his, w_los = [], [], [], []
        for v in (v0, v0 + 1):
            parts = []
            for p, q in ((gxa, gxb), (gya, gyb)):
                for f in (nv, nv + 1):
                    parts.append(split(p[v] * p[f]))
                    parts.append(split(q[v] * q[f]))
            highs.append(jnp.concatenate([p[0] for p in parts], axis=0))
            lows.append(jnp.concatenate([p[1] for p in parts], axis=0))
            w_his.append(jnp.where(group_of == v, tile_hi, 0.0).astype(bf16))
            w_los.append(jnp.where(group_of == v, tile_lo, 0.0).astype(bf16))
        hi, lo = jnp.concatenate(highs, axis=1), jnp.concatenate(lows, axis=1)
        w_hi, w_lo = jnp.concatenate(w_his, axis=1), jnp.concatenate(w_los, axis=1)
        t = mm(edge[:, : 3 * EDGE], jnp.concatenate([hi, lo, hi], axis=0))
        t = t + mm(z_hi, w_hi) + mm(z_lo, w_hi) + mm(z_hi, w_lo)
        for q in range(2):
            out[v0 + q] = base[v0 + q] + t[:, q * 128 : q * 128 + 128]
        at = slice(v0, v0 + 2)
        c = pltpu.make_async_copy(out.at[at], final.at[at], sem_out.at[v0 // 2])
        c.start()
        outs.append(c)
    for c in outs:
        c.wait()


def call_finish(base, edge, faces, rows):
    nv = base.shape[0] - 2
    return pl.pallas_call(
        finish,
        out_shape=(
            jax.ShapeDtypeStruct((nv, 256, 128), f32),
            jax.ShapeDtypeStruct((1, 128), f32),
        ),
        in_specs=[vm] * 6 + [hbm] * 3,
        out_specs=(hbm, vm),
        scratch_shapes=[
            pltpu.VMEM((128, 128), f32),
            pltpu.VMEM((128, 128), f32),
            pltpu.VMEM(rows.shape, f32),
            pltpu.VMEM((nv, 256, 128), f32),
            pltpu.SemaphoreType.DMA((3,)),
            pltpu.SemaphoreType.DMA((nv // 2,)),
        ],
        compiler_params=params(16),
        cost_estimate=cost(2 << 30, 6),
        name="finish",
    )(
        *(in_vmem(x) for x in (base, edge, *faces[:4])), *(in_hbm(x) for x in (*faces[4:], rows))
    )


def shards(
    adjoint_in,
    velocity,
    viscosity,
    rate,
    chemistry,
    stencil_x,
    stencil_y,
    stencil_z,
    sensitivity,
    patch_ids,
):
    nv = adjoint_in.shape[0]
    assert adjoint_in.shape[1:] == (16, 16, 128) and nv == 14 and sensitivity.shape[0] == 128
    devices = lax.axis_size("gx") * lax.axis_size("gy") * lax.axis_size("gz")
    adj, vel = adjoint_in.reshape(nv, 256, 128), velocity.reshape(3, 256, 128)
    gya, gyb, fields = call_pack_y(adj, vel, viscosity.reshape(256, 128))
    gya, gyb = swap(gya, gyb, "gy")
    gxa, gxb, gza, gzb, contrib = call_pack_xz(
        patch_ids, fields, vel, sensitivity, devices
    )
    gxa, gxb = swap(gxa, gxb, "gx")
    gza, gzb = swap(gza, gzb, "gz")
    rows = lax.all_to_all(contrib, AXES, 0, 0, tiled=True)
    base, edge = call_interior(
        chemistry,
        fields,
        vel,
        rate.reshape(256, 128),
        stencil_x,
        stencil_y,
        jnp.swapaxes(stencil_z, 1, 2),
    )
    faces = (gxa, gxb, gya, gyb, gza, gzb)
    out, grad = call_finish(base, edge, faces, rows)
    return out.reshape(adjoint_in.shape), grad


def solution(mesh):
    return jax.shard_map(
        shards,
        mesh=mesh,
        in_specs=(
            P(None, "gx", "gy", "gz"),
            P(None, "gx", "gy", "gz"),
            P("gx", "gy", "gz"),
            P("gx", "gy", "gz"),
            P(),
            P(),
            P(),
            P(),
            P(None, "gx", "gz"),
            P("gx", "gy", "gz"),
        ),
        out_specs=(P(None, "gx", "gy", "gz"), P(("gx", "gy", "gz"), None)),
        check_vma=False,
    )
```

time: 403 us -> 48 us (0.12); the launches traced: 397 us -> 47.8 us
  waiting for transfers between devices: 264 us -> 2.78 us
  other arithmetic: 34.9 us -> 0 us
  matrix products: 32.3 us -> 0 us
  local copies, waits for them, and re-layouts: 31.1 us -> 0.63 us
  Pallas kernels: 0 us -> 17.9 us
  between operations: 15.3 us -> 1.53 us
  starting transfers between devices: 19.3 us -> 24.9 us
    unnamed x2 -> x0, waiting for transfers between devices: 240 us -> none
    dot_general x8 -> x0, matrix products: 32.3 us -> none  [the longest x3 14.8 us: apply_dir(): first = jnp.einsum(form, stencil[0], advected, precision=highest)]
    concatenate x3 -> x0, other arithmetic: 24.3 us -> none  [extended(): x = jnp.concatenate([before, x, after], axis=dim)]
    ppermute x6, waiting for transfers between devices: 23.8 us -> 1.13 us  [swap(): return (lax.ppermute(a, axis, plan_a), lax.ppermute(b, axis, plan_b))]
    pallas_call x0 -> x4, Pallas kernels: none -> 17.9 us  [the longest x1 6.44 us: call_interior(): pl.pallas_call(interior, out_shape=(resident(nv + 2, 256, 128), resident(...]
    slice x5 -> x0, local copies, waits for them, and re-layouts: 16.6 us -> none  [the longest x3 11.3 us: extended(): last = lax.slice_in_dim(x, length - width, length, axis=dim)]
    ppermute x4 -> x0, local copies, waits for them, and re-layouts: 10.9 us -> none  [the longest x2 5.47 us: extended(): after = lax.ppermute(leading, axis, down)]
    all_to_all x0 -> x1, starting transfers between devices: none -> 10.1 us  [shards(): rows = lax.all_to_all(contrib, AXES, 0, 0, tiled=True)]
  transfers between devices with their start and end apart: 7 -> 7, of which waited for: 2 -> 2; matrix products, arithmetic and copies ran while one was open for 9% -> 0% of each run, Pallas kernels for 0% -> 19%
where the time goes in v2:
time: 48 us; the launch traced here: 47.8 us
  starting transfers between devices  24.9 us (52%)
  Pallas kernels  17.9 us (37%)
  waiting for transfers between devices  2.78 us (6%)
  between operations  1.53 us (3%)
  local copies, waits for them, and re-layouts  0.63 us (1%)
    ppermute x6, starting transfers between devices, swap(): return (lax.ppermute(a, axis, plan_a), lax.ppermute(b, axis, plan_b))  14.8 us
    all_to_all x1, starting transfers between devices, shards(): rows = lax.all_to_all(contrib, AXES, 0, 0, tiled=True)  10.1 us
    pallas_call x1, Pallas kernels, call_interior(): pl.pallas_call(interior, out_shape=(resident(nv + 2, 256, 128), resident(...  6.44 us
    pallas_call x1, Pallas kernels, call_finish(): pl.pallas_call(finish, out_shape=(jax.ShapeDtypeStruct((nv, 256, 128), f3...  6.43 us
    pallas_call x1, Pallas kernels, call_pack_xz(): pl.pallas_call(pack_xz, out_shape=(gx, gx, gz, gz, jax.ShapeDtypeStruct((...  2.56 us
    pallas_call x1, Pallas kernels, call_pack_y(): pl.pallas_call(pack_y, out_shape=(gy, gy, resident(nv + 2, 256, 128)), in...  2.5 us
    all_to_all x1, waiting for transfers between devices, shards(): rows = lax.all_to_all(contrib, AXES, 0, 0, tiled=True)  1.66 us
    ppermute x6, waiting for transfers between devices, swap(): return (lax.ppermute(a, axis, plan_a), lax.ppermute(b, axis, plan_b))  1.13 us
  transfers between devices with their start and end apart: 7, of which 2 were waited for; matrix products, arithmetic and copies ran while one was open for 0% of the time, Pallas kernels for 19%

profile of v2, /device:TPU:1, one launch (start us, length us, event | category | flops | bytes accessed | tf_op | source)
XLA Modules:
  0.0 47.8 jit_solution(4485406190161559213)
XLA Ops:
  0.6 0.0 copy-start
  0.6 0.0 copy-start.1
  0.7 2.5 %pack_y.1 = (f32[16,64,128]{2,1,0:T(8,128)}, f32[16,64,128]{2,1,0:T(8,128)}, f32[16,256,128]{2,1,0:T(8,128)S(1)}) custom-call(f32[14,256,128]{2,1,0:T(8,128)} %bitcast.13, f32[3,256,128]{2,1,0:T(8,128)} %bitcast.10, f32[256,128]{1,0:T(8,128)} %bitcast.15), custom_call_target="tpu_custom_call" | custom-call | flops 1 | bytes 1024 | tf_op jit(solution)/shard_map/pack_y/pallas_call | solution.py:101
  3.2 3.8 %collective-permute-start.2 = (f32[16,64,128]{2,1,0:T(8,128)}, f32[16,64,128]{2,1,0:T(8,128)S(1)}, u32[]{:S(2)}, u32[]{:S(2)}) collective-permute-start(f32[16,64,128]{2,1,0:T(8,128)} %get-tuple-element.19), channel_id=1, source_target_pairs={{0,4},{4,0},{8,12},{12,8},{16,20},{20,16},{24,28},{28,24},{1,5},{5... | collective-permute-start | bytes 1572872 | tf_op jit(solution)/shard_map/ppermute | solution.py:20
  7.0 2.3 %collective-permute-start.3 = (f32[16,64,128]{2,1,0:T(8,128)}, f32[16,64,128]{2,1,0:T(8,128)}, u32[]{:S(2)}, u32[]{:S(2)}) collective-permute-start(f32[16,64,128]{2,1,0:T(8,128)} %get-tuple-element.20), channel_id=1, source_target_pairs={{0,28},{4,8},{8,4},{12,16},{16,12},{20,24},{24,20},{28,0},{1,29},{... | collective-permute-start | bytes 1572872 | tf_op jit(solution)/shard_map/ppermute | solution.py:20
  9.9 0.0 copy-done
  9.9 0.0 copy-done.1
  10.0 2.6 %pack_xz.1 = (f32[16,64,128]{2,1,0:T(8,128)}, f32[16,64,128]{2,1,0:T(8,128)}, f32[128,128]{1,0:T(8,128)}, f32[128,128]{1,0:T(8,128)}, f32[256,128]{1,0:T(8,128)}) custom-call(s32[1,1,1]{2,1,0:T(1,128)S(6)} %copy.15.ids, f32[16,256,128]{2,1,0:T(8,128)S(1)} %get-tuple-element.14.fields, f32[3,256,128]{2,1,0:T(8,128)S(1)} %bitcast.12, f32[128,16,128]{2,1,0:T(8,128)S(1)} %copy-done.1), custom_call_target="tpu_custom_call" | custom-call | flops 1 | bytes 1024 | tf_op jit(solution)/shard_map/pack_xz/pallas_call | solution.py:174
  12.5 1.7 %collective-permute-start = (f32[16,64,128]{2,1,0:T(8,128)}, f32[16,64,128]{2,1,0:T(8,128)}, u32[]{:S(2)}, u32[]{:S(2)}) collective-permute-start(f32[16,64,128]{2,1,0:T(8,128)} %get-tuple-element.17), channel_id=1, source_target_pairs={{0,32},{32,0},{64,96},{96,64},{128,160},{160,128},{192,224},{224,1... | collective-permute-start | bytes 1572872 | tf_op jit(solution)/shard_map/ppermute | solution.py:20
  14.3 4.7 %collective-permute-start.1 = (f32[16,64,128]{2,1,0:T(8,128)}, f32[16,64,128]{2,1,0:T(8,128)}, u32[]{:S(2)}, u32[]{:S(2)}) collective-permute-start(f32[16,64,128]{2,1,0:T(8,128)} %get-tuple-element.18), channel_id=1, source_target_pairs={{0,224},{32,64},{64,32},{96,128},{128,96},{160,192},{192,160},{224... | collective-permute-start | bytes 1572872 | tf_op jit(solution)/shard_map/ppermute | solution.py:20
  18.9 10.1 %all-to-all-start = ((f32[256,1,128]{2,1,0:T(1,128)}), f32[256,1,128]{2,1,0:T(1,128)}, u32[]{:S(2)}, u32[]{:S(2)}) async-start(f32[256,1,128]{2,1,0:T(1,128)} %bitcast.6), calls=%async_computation | async-start | bytes 262144 | tf_op jit(solution)/shard_map/all_to_all | solution.py:501
  29.0 2.3 %collective-permute-start.4 = (f32[128,128]{1,0:T(8,128)}, f32[128,128]{1,0:T(8,128)S(1)}, u32[]{:S(2)}, u32[]{:S(2)}) collective-permute-start(f32[128,128]{1,0:T(8,128)} %get-tuple-element.21), channel_id=1, source_target_pairs={{0,1},{1,0},{2,3},{3,2},{4,5},{5,4},{6,7},{7,6},{8,9},{9,8},{10,11... | collective-permute-start | bytes 196616 | tf_op jit(solution)/shard_map/ppermute | solution.py:20
  31.3 1.1 %collective-permute-done.4.gza_in = f32[128,128]{1,0:T(8,128)S(1)} collective-permute-done((f32[128,128]{1,0:T(8,128)}, f32[128,128]{1,0:T(8,128)S(1)}, u32[]{:S(2)}, u32[]{:S(2)}) %collective-permute-start.4) | collective-permute-done | bytes 65568 | tf_op jit(solution)/shard_map/ppermute | solution.py:20
  32.4 0.0 copy-start.2
  32.4 0.0 collective-permute-start.5
  32.4 0.6 %copy-done.2 = f32[128,128]{1,0:T(8,128)} copy-done((f32[128,128]{1,0:T(8,128)}, f32[128,128]{1,0:T(8,128)S(1)}, u32[]{:S(2)}) %copy-start.2) | copy-done | bytes 65560
  33.0 6.4 %interior.1 = (f32[16,256,128]{2,1,0:T(8,128)S(1)}, bf16[256,1792]{1,0:T(8,128)(2,1)S(1)}) custom-call(f32[14,14]{1,0:T(8,128)} %chem_in.1, f32[16,256,128]{2,1,0:T(8,128)S(1)} %get-tuple-element.14.fields, f32[3,256,128]{2,1,0:T(8,128)} %bitcast.11, f32[256,128]{1,0:T(8,128)} %bitcast.16, f32[2,16,24]{2,1,0:T(8,128)} %sx_in.1, ...), custom_call_target="tpu_custom_call", output_to_operand_aliasing={{0}: (1, {})} | custom-call | flops 1 | bytes 1024 | tf_op jit(solution)/shard_map/interior/pallas_call | solution.py:362
  39.5 0.0 collective-permute-done.5.gzb_in
  39.5 1.7 %all-to-all-done = f32[256,1,128]{2,1,0:T(1,128)} async-done(((f32[256,1,128]{2,1,0:T(1,128)}), f32[256,1,128]{2,1,0:T(1,128)}, u32[]{:S(2)}, u32[]{:S(2)}) %all-to-all-start) | async-done | bytes 131104 | tf_op jit(solution)/shard_map/all_to_all | solution.py:501
  41.2 0.0 collective-permute-done.2.gya
  41.2 0.0 collective-permute-done.3.gyb
  41.2 0.0 collective-permute-done.gxa
  41.2 0.0 collective-permute-done.1.gxb
  41.2 6.4 %finish.1 = (f32[14,256,128]{2,1,0:T(8,128)}, f32[1,128]{1,0:T(1,128)}) custom-call(f32[16,256,128]{2,1,0:T(8,128)S(1)} %get-tuple-element.15.base, bf16[256,1792]{1,0:T(8,128)(2,1)S(1)} %get-tuple-element.16.edge, f32[16,64,128]{2,1,0:T(8,128)} %collective-permute-done.gxa, f32[16,64,128]{2,1,0:T(8,128)} %collective-permute-done.1.gxb, ...), custom_call_target="tpu_custom_call" | custom-call | flops 1 | bytes 1024 | tf_op jit(solution)/shard_map/finish/pallas_call | solution.py:454
Async XLA Ops:
  0.6 9.3 %copy-start = (f32[3,16,16,128]{3,2,1,0:T(8,128)S(1)}, f32[3,16,16,128]{3,2,1,0:T(8,128)}, u32[]{:S(2)}) copy-start(f32[3,16,16,128]{3,2,1,0:T(8,128)} %param.11) | copy-start | bytes 1179652
  0.6 9.3 %copy-start.1 = (f32[128,16,128]{2,1,0:T(8,128)S(1)}, f32[128,16,128]{2,1,0:T(8,128)}, u32[]{:S(2)}) copy-start(f32[128,16,128]{2,1,0:T(8,128)} %sens.1) | copy-start | bytes 3145732
  3.2 38.0 %collective-permute-start.2 = (f32[16,64,128]{2,1,0:T(8,128)}, f32[16,64,128]{2,1,0:T(8,128)S(1)}, u32[]{:S(2)}, u32[]{:S(2)}) collective-permute-start(f32[16,64,128]{2,1,0:T(8,128)} %get-tuple-element.19), channel_id=1, source_target_pairs={{0,4},{4,0},{8,12},{12,8},{16,20},{20,16},{24,28},{28,24},{1,5},{5... | collective-permute-start | bytes 1572872 | tf_op jit(solution)/shard_map/ppermute | solution.py:20
  7.0 34.2 %collective-permute-start.3 = (f32[16,64,128]{2,1,0:T(8,128)}, f32[16,64,128]{2,1,0:T(8,128)}, u32[]{:S(2)}, u32[]{:S(2)}) collective-permute-start(f32[16,64,128]{2,1,0:T(8,128)} %get-tuple-element.20), channel_id=1, source_target_pairs={{0,28},{4,8},{8,4},{12,16},{16,12},{20,24},{24,20},{28,0},{1,29},{... | collective-permute-start | bytes 1572872 | tf_op jit(solution)/shard_map/ppermute | solution.py:20
  12.5 28.6 %collective-permute-start = (f32[16,64,128]{2,1,0:T(8,128)}, f32[16,64,128]{2,1,0:T(8,128)}, u32[]{:S(2)}, u32[]{:S(2)}) collective-permute-start(f32[16,64,128]{2,1,0:T(8,128)} %get-tuple-element.17), channel_id=1, source_target_pairs={{0,32},{32,0},{64,96},{96,64},{128,160},{160,128},{192,224},{224,1... | collective-permute-start | bytes 1572872 | tf_op jit(solution)/shard_map/ppermute | solution.py:20
  14.3 26.9 %collective-permute-start.1 = (f32[16,64,128]{2,1,0:T(8,128)}, f32[16,64,128]{2,1,0:T(8,128)}, u32[]{:S(2)}, u32[]{:S(2)}) collective-permute-start(f32[16,64,128]{2,1,0:T(8,128)} %get-tuple-element.18), channel_id=1, source_target_pairs={{0,224},{32,64},{64,32},{96,128},{128,96},{160,192},{192,160},{224... | collective-permute-start | bytes 1572872 | tf_op jit(solution)/shard_map/ppermute | solution.py:20
  18.9 22.2 %all-to-all-start = ((f32[256,1,128]{2,1,0:T(1,128)}), f32[256,1,128]{2,1,0:T(1,128)}, u32[]{:S(2)}, u32[]{:S(2)}) async-start(f32[256,1,128]{2,1,0:T(1,128)} %bitcast.6), calls=%async_computation | async-start | bytes 262144 | tf_op jit(solution)/shard_map/all_to_all | solution.py:501
  29.0 3.4 %collective-permute-start.4 = (f32[128,128]{1,0:T(8,128)}, f32[128,128]{1,0:T(8,128)S(1)}, u32[]{:S(2)}, u32[]{:S(2)}) collective-permute-start(f32[128,128]{1,0:T(8,128)} %get-tuple-element.21), channel_id=1, source_target_pairs={{0,1},{1,0},{2,3},{3,2},{4,5},{5,4},{6,7},{7,6},{8,9},{9,8},{10,11... | collective-permute-start | bytes 196616 | tf_op jit(solution)/shard_map/ppermute | solution.py:20
  32.4 0.6 %copy-start.2 = (f32[128,128]{1,0:T(8,128)}, f32[128,128]{1,0:T(8,128)S(1)}, u32[]{:S(2)}) copy-start(f32[128,128]{1,0:T(8,128)S(1)} %collective-permute-done.4.gza_in) | copy-start | bytes 196612
  32.4 7.1 %collective-permute-start.5 = (f32[128,128]{1,0:T(8,128)}, f32[128,128]{1,0:T(8,128)}, u32[]{:S(2)}, u32[]{:S(2)}) collective-permute-start(f32[128,128]{1,0:T(8,128)} %get-tuple-element.22), channel_id=1, source_target_pairs={{0,3},{1,2},{2,1},{3,0},{4,7},{5,6},{6,5},{7,4},{8,11},{9,10},{10,... | collective-permute-start | bytes 196616 | tf_op jit(solution)/shard_map/ppermute | solution.py:20

commit v3 on v2

--- a/solution.py
+++ b/solution.py
@@ -296,6 +296,9 @@
             out[:, at : at + 16, :] = t[:, 128 * q : 128 * q + 128].reshape(nv, 16, 128)
 
 
+ARRIVE = ((12, 16), (0, 4), (4, 8), (8, 12))
+
+
 def spread(face, lane, group):
     x = jnp.where(lane >> 3 == group, face, 0.0)
     for shift in (64, 32, 16, 8):
@@ -320,9 +323,10 @@
     ins = [pltpu.make_async_copy(src, dst, sem_in.at[k]) for k, (src, dst) in enumerate(copies)]
     for c in ins:
         c.start()
-    for c in ins:
-        c.wait()
+    ins[2].wait()
+    ins[3].wait()
     build_matrices(sx, sy, matrix, edge)
+    ins[4].wait()
     index, n = lax.axis_index("gz"), lax.axis_size("gz")
     has_before = jnp.where(index > 0, 1.0, 0.0)
     has_after = jnp.where(index < n - 1, 1.0, 0.0)
@@ -337,7 +341,11 @@
         hi, lo = split(jnp.concatenate([ends] * 16, axis=0))
         edge[f * 128 : f * 128 + 128, 3 * EDGE : 3 * EDGE + 128] = hi
         edge[f * 128 : f * 128 + 128, 3 * EDGE + 128 :] = lo
+    ins[0].wait()
+    ins[1].wait()
     react(chem, fields, rate, out, x_hi, x_lo)
+    ins[5].wait()
+    ins[6].wait()
     for v0 in range(0, nv, 2):
         highs, lows, zs = [], [], []
         for v in (v0, v0 + 1):
@@ -391,8 +399,8 @@
 
 
 def finish(
-    base, edge, gxa, gxb, gya, gyb, gza_in, gzb_in, rows_in, final, grad,
-    gza, gzb, rows, out, sem_in, sem_out,
+    base, edge, gxa_in, gxb_in, gya_in, gyb_in, gza_in, gzb_in, rows_in, final, grad,
+    gxa, gxb, gya, gyb, gza, gzb, rows, out, sem_in, sem_face, sem_out,
 ):
     nv = out.shape[0]
     ins = [
@@ -401,9 +409,19 @@
     ]
     for c in ins:
         c.start()
-    for c in ins:
-        c.wait()
-    grad[...] = section_step * jnp.sum(rows[...], axis=0, keepdims=True)
+    groups = []
+    pairs = ((gxa_in, gxa), (gxb_in, gxb), (gya_in, gya), (gyb_in, gyb))
+    for k, (c0, c1) in enumerate(ARRIVE):
+        groups.append(
+            [
+                pltpu.make_async_copy(src.at[c0:c1], dst.at[c0:c1], sem_face.at[k, q])
+                for q, (src, dst) in enumerate(pairs)
+            ]
+        )
+        for c in groups[-1]:
+            c.start()
+    ins[0].wait()
+    ins[1].wait()
     even = is_even("gz")
     before = jnp.where(even, gzb[...], gza[...])
     after = jnp.where(even, gza[...], gzb[...])
@@ -423,7 +441,11 @@
     tile_hi = edge[:, 3 * EDGE : 3 * EDGE + 128].astype(f32)
     tile_lo = edge[:, 3 * EDGE + 128 :].astype(f32)
     outs = []
-    for v0 in range(0, nv, 2):
+    for v0 in (nv - 2, *range(0, nv - 2, 2)):
+        for k, (c0, c1) in enumerate(ARRIVE):
+            if v0 == c0:
+                for c in groups[k]:
+                    c.wait()
         highs, lows, w_his, w_los = [], [], [], []
         for v in (v0, v0 + 1):
             parts = []
@@ -445,6 +467,8 @@
         c = pltpu.make_async_copy(out.at[at], final.at[at], sem_out.at[v0 // 2])
         c.start()
         outs.append(c)
+    ins[2].wait()
+    grad[...] = section_step * jnp.sum(rows[...], axis=0, keepdims=True)
     for c in outs:
         c.wait()
 
@@ -457,21 +481,23 @@
             jax.ShapeDtypeStruct((nv, 256, 128), f32),
             jax.ShapeDtypeStruct((1, 128), f32),
         ),
-        in_specs=[vm] * 6 + [hbm] * 3,
+        in_specs=[vm] * 2 + [hbm] * 7,
         out_specs=(hbm, vm),
         scratch_shapes=[
+            *[pltpu.VMEM((nv + 2, 64, 128), f32)] * 4,
             pltpu.VMEM((128, 128), f32),
             pltpu.VMEM((128, 128), f32),
             pltpu.VMEM(rows.shape, f32),
             pltpu.VMEM((nv, 256, 128), f32),
             pltpu.SemaphoreType.DMA((3,)),
+            pltpu.SemaphoreType.DMA((len(ARRIVE), 4)),
             pltpu.SemaphoreType.DMA((nv // 2,)),
         ],
         compiler_params=params(16),
         cost_estimate=cost(2 << 30, 6),
         name="finish",
     )(
-        *(in_vmem(x) for x in (base, edge, *faces[:4])), *(in_hbm(x) for x in (*faces[4:], rows))
+        in_vmem(base), in_vmem(edge), *faces[:4], *(in_hbm(x) for x in (*faces[4:], rows))
     )
 
 

time: 48 us -> 47.3 us (0.985)
    pallas_call x1, Pallas kernels: 6.43 us -> 5.8 us  [call_finish(): pl.pallas_call(finish, out_shape=(jax.ShapeDtypeStruct((nv, 256, 128), f3...]
  transfers between devices with their start and end apart: 7 -> 7, of which waited for: 2 -> 2; matrix products, arithmetic and copies ran while one was open for 0% -> 0% of each run, Pallas kernels for 19% -> 20%
where the time goes in v3:
time: 47.3 us; the launch traced here: 47.1 us
  starting transfers between devices  24.9 us (53%)
  Pallas kernels  17.6 us (37%)
  waiting for transfers between devices  2.49 us (5%)
  between operations  1.53 us (3%)
  local copies, waits for them, and re-layouts  0.63 us (1%)
    ppermute x6, starting transfers between devices, swap(): return (lax.ppermute(a, axis, plan_a), lax.ppermute(b, axis, plan_b))  14.8 us
    all_to_all x1, starting transfers between devices, shards(): rows = lax.all_to_all(contrib, AXES, 0, 0, tiled=True)  10.1 us
    pallas_call x1, Pallas kernels, call_interior(): pl.pallas_call(interior, out_shape=(resident(nv + 2, 256, 128), resident(...  6.73 us
    pallas_call x1, Pallas kernels, call_finish(): pl.pallas_call(finish, out_shape=(jax.ShapeDtypeStruct((nv, 256, 128), f3...  5.8 us
    pallas_call x1, Pallas kernels, call_pack_xz(): pl.pallas_call(pack_xz, out_shape=(gx, gx, gz, gz, jax.ShapeDtypeStruct((...  2.56 us
    pallas_call x1, Pallas kernels, call_pack_y(): pl.pallas_call(pack_y, out_shape=(gy, gy, resident(nv + 2, 256, 128)), in...  2.5 us
    all_to_all x1, waiting for transfers between devices, shards(): rows = lax.all_to_all(contrib, AXES, 0, 0, tiled=True)  1.36 us
    ppermute x6, waiting for transfers between devices, swap(): return (lax.ppermute(a, axis, plan_a), lax.ppermute(b, axis, plan_b))  1.13 us
  transfers between devices with their start and end apart: 7, of which 2 were waited for; matrix products, arithmetic and copies ran while one was open for 0% of the time, Pallas kernels for 20%

profile of v3, /device:TPU:1, one launch (start us, length us, event | category | flops | bytes accessed | tf_op | source)
XLA Modules:
  0.0 47.1 jit_solution(9146406017043478920)
XLA Ops:
  0.6 0.0 copy-start
  0.6 0.0 copy-start.1
  0.7 2.5 %pack_y.1 = (f32[16,64,128]{2,1,0:T(8,128)}, f32[16,64,128]{2,1,0:T(8,128)}, f32[16,256,128]{2,1,0:T(8,128)S(1)}) custom-call(f32[14,256,128]{2,1,0:T(8,128)} %bitcast.13, f32[3,256,128]{2,1,0:T(8,128)} %bitcast.10, f32[256,128]{1,0:T(8,128)} %bitcast.15), custom_call_target="tpu_custom_call" | custom-call | flops 1 | bytes 1024 | tf_op jit(solution)/shard_map/pack_y/pallas_call | solution.py:101
  3.2 3.8 %collective-permute-start.2 = (f32[16,64,128]{2,1,0:T(8,128)}, f32[16,64,128]{2,1,0:T(8,128)S(1)}, u32[]{:S(2)}, u32[]{:S(2)}) collective-permute-start(f32[16,64,128]{2,1,0:T(8,128)} %get-tuple-element.19), channel_id=1, source_target_pairs={{0,4},{4,0},{8,12},{12,8},{16,20},{20,16},{24,28},{28,24},{1,5},{5... | collective-permute-start | bytes 1572872 | tf_op jit(solution)/shard_map/ppermute | solution.py:20
  7.0 2.3 %collective-permute-start.3 = (f32[16,64,128]{2,1,0:T(8,128)}, f32[16,64,128]{2,1,0:T(8,128)}, u32[]{:S(2)}, u32[]{:S(2)}) collective-permute-start(f32[16,64,128]{2,1,0:T(8,128)} %get-tuple-element.20), channel_id=1, source_target_pairs={{0,28},{4,8},{8,4},{12,16},{16,12},{20,24},{24,20},{28,0},{1,29},{... | collective-permute-start | bytes 1572872 | tf_op jit(solution)/shard_map/ppermute | solution.py:20
  9.9 0.0 copy-done
  9.9 0.0 copy-done.1
  10.0 2.6 %pack_xz.1 = (f32[16,64,128]{2,1,0:T(8,128)}, f32[16,64,128]{2,1,0:T(8,128)}, f32[128,128]{1,0:T(8,128)}, f32[128,128]{1,0:T(8,128)}, f32[256,128]{1,0:T(8,128)}) custom-call(s32[1,1,1]{2,1,0:T(1,128)S(6)} %copy.15.ids, f32[16,256,128]{2,1,0:T(8,128)S(1)} %get-tuple-element.14.fields, f32[3,256,128]{2,1,0:T(8,128)S(1)} %bitcast.12, f32[128,16,128]{2,1,0:T(8,128)S(1)} %copy-done.1), custom_call_target="tpu_custom_call" | custom-call | flops 1 | bytes 1024 | tf_op jit(solution)/shard_map/pack_xz/pallas_call | solution.py:174
  12.5 1.7 %collective-permute-start = (f32[16,64,128]{2,1,0:T(8,128)}, f32[16,64,128]{2,1,0:T(8,128)}, u32[]{:S(2)}, u32[]{:S(2)}) collective-permute-start(f32[16,64,128]{2,1,0:T(8,128)} %get-tuple-element.17), channel_id=1, source_target_pairs={{0,32},{32,0},{64,96},{96,64},{128,160},{160,128},{192,224},{224,1... | collective-permute-start | bytes 1572872 | tf_op jit(solution)/shard_map/ppermute | solution.py:20
  14.3 4.7 %collective-permute-start.1 = (f32[16,64,128]{2,1,0:T(8,128)}, f32[16,64,128]{2,1,0:T(8,128)}, u32[]{:S(2)}, u32[]{:S(2)}) collective-permute-start(f32[16,64,128]{2,1,0:T(8,128)} %get-tuple-element.18), channel_id=1, source_target_pairs={{0,224},{32,64},{64,32},{96,128},{128,96},{160,192},{192,160},{224... | collective-permute-start | bytes 1572872 | tf_op jit(solution)/shard_map/ppermute | solution.py:20
  18.9 10.1 %all-to-all-start = ((f32[256,1,128]{2,1,0:T(1,128)}), f32[256,1,128]{2,1,0:T(1,128)}, u32[]{:S(2)}, u32[]{:S(2)}) async-start(f32[256,1,128]{2,1,0:T(1,128)} %bitcast.6), calls=%async_computation | async-start | bytes 262144 | tf_op jit(solution)/shard_map/all_to_all | solution.py:527
  29.0 2.3 %collective-permute-start.4 = (f32[128,128]{1,0:T(8,128)}, f32[128,128]{1,0:T(8,128)S(1)}, u32[]{:S(2)}, u32[]{:S(2)}) collective-permute-start(f32[128,128]{1,0:T(8,128)} %get-tuple-element.21), channel_id=1, source_target_pairs={{0,1},{1,0},{2,3},{3,2},{4,5},{5,4},{6,7},{7,6},{8,9},{9,8},{10,11... | collective-permute-start | bytes 196616 | tf_op jit(solution)/shard_map/ppermute | solution.py:20
  31.3 1.1 %collective-permute-done.4.gza_in = f32[128,128]{1,0:T(8,128)S(1)} collective-permute-done((f32[128,128]{1,0:T(8,128)}, f32[128,128]{1,0:T(8,128)S(1)}, u32[]{:S(2)}, u32[]{:S(2)}) %collective-permute-start.4) | collective-permute-done | bytes 65568 | tf_op jit(solution)/shard_map/ppermute | solution.py:20
  32.4 0.0 copy-start.2
  32.4 0.0 collective-permute-start.5
  32.4 0.6 %copy-done.2 = f32[128,128]{1,0:T(8,128)} copy-done((f32[128,128]{1,0:T(8,128)}, f32[128,128]{1,0:T(8,128)S(1)}, u32[]{:S(2)}) %copy-start.2) | copy-done | bytes 65560
  33.0 6.7 %interior.1 = (f32[16,256,128]{2,1,0:T(8,128)S(1)}, bf16[256,1792]{1,0:T(8,128)(2,1)S(1)}) custom-call(f32[14,14]{1,0:T(8,128)} %chem_in.1, f32[16,256,128]{2,1,0:T(8,128)S(1)} %get-tuple-element.14.fields, f32[3,256,128]{2,1,0:T(8,128)} %bitcast.11, f32[256,128]{1,0:T(8,128)} %bitcast.16, f32[2,16,24]{2,1,0:T(8,128)} %sx_in.1, ...), custom_call_target="tpu_custom_call", output_to_operand_aliasing={{0}: (1, {})} | custom-call | flops 1 | bytes 1024 | tf_op jit(solution)/shard_map/interior/pallas_call | solution.py:370
  39.8 0.0 collective-permute-done.5.gzb_in
  39.8 1.4 %all-to-all-done = f32[256,1,128]{2,1,0:T(1,128)} async-done(((f32[256,1,128]{2,1,0:T(1,128)}), f32[256,1,128]{2,1,0:T(1,128)}, u32[]{:S(2)}, u32[]{:S(2)}) %all-to-all-start) | async-done | bytes 131104 | tf_op jit(solution)/shard_map/all_to_all | solution.py:527
  41.2 0.0 collective-permute-done.2.gya_in
  41.2 0.0 collective-permute-done.3.gyb_in
  41.2 0.0 collective-permute-done.gxa_in
  41.2 0.0 collective-permute-done.1.gxb_in
  41.2 5.8 %finish.1 = (f32[14,256,128]{2,1,0:T(8,128)}, f32[1,128]{1,0:T(1,128)}) custom-call(f32[16,256,128]{2,1,0:T(8,128)S(1)} %get-tuple-element.15.base, bf16[256,1792]{1,0:T(8,128)(2,1)S(1)} %get-tuple-element.16.edge, f32[16,64,128]{2,1,0:T(8,128)} %collective-permute-done.gxa_in, f32[16,64,128]{2,1,0:T(8,128)} %collective-permute-done.1.gxb_in, ...), custom_call_target="tpu_custom_call" | custom-call | flops 1 | bytes 1024 | tf_op jit(solution)/shard_map/finish/pallas_call | solution.py:478
Async XLA Ops:
  0.6 9.3 %copy-start = (f32[3,16,16,128]{3,2,1,0:T(8,128)S(1)}, f32[3,16,16,128]{3,2,1,0:T(8,128)}, u32[]{:S(2)}) copy-start(f32[3,16,16,128]{3,2,1,0:T(8,128)} %param.11) | copy-start | bytes 1179652
  0.6 9.3 %copy-start.1 = (f32[128,16,128]{2,1,0:T(8,128)S(1)}, f32[128,16,128]{2,1,0:T(8,128)}, u32[]{:S(2)}) copy-start(f32[128,16,128]{2,1,0:T(8,128)} %sens.1) | copy-start | bytes 3145732
  3.2 38.0 %collective-permute-start.2 = (f32[16,64,128]{2,1,0:T(8,128)}, f32[16,64,128]{2,1,0:T(8,128)S(1)}, u32[]{:S(2)}, u32[]{:S(2)}) collective-permute-start(f32[16,64,128]{2,1,0:T(8,128)} %get-tuple-element.19), channel_id=1, source_target_pairs={{0,4},{4,0},{8,12},{12,8},{16,20},{20,16},{24,28},{28,24},{1,5},{5... | collective-permute-start | bytes 1572872 | tf_op jit(solution)/shard_map/ppermute | solution.py:20
  7.0 34.2 %collective-permute-start.3 = (f32[16,64,128]{2,1,0:T(8,128)}, f32[16,64,128]{2,1,0:T(8,128)}, u32[]{:S(2)}, u32[]{:S(2)}) collective-permute-start(f32[16,64,128]{2,1,0:T(8,128)} %get-tuple-element.20), channel_id=1, source_target_pairs={{0,28},{4,8},{8,4},{12,16},{16,12},{20,24},{24,20},{28,0},{1,29},{... | collective-permute-start | bytes 1572872 | tf_op jit(solution)/shard_map/ppermute | solution.py:20
  12.5 28.6 %collective-permute-start = (f32[16,64,128]{2,1,0:T(8,128)}, f32[16,64,128]{2,1,0:T(8,128)}, u32[]{:S(2)}, u32[]{:S(2)}) collective-permute-start(f32[16,64,128]{2,1,0:T(8,128)} %get-tuple-element.17), channel_id=1, source_target_pairs={{0,32},{32,0},{64,96},{96,64},{128,160},{160,128},{192,224},{224,1... | collective-permute-start | bytes 1572872 | tf_op jit(solution)/shard_map/ppermute | solution.py:20
  14.3 26.9 %collective-permute-start.1 = (f32[16,64,128]{2,1,0:T(8,128)}, f32[16,64,128]{2,1,0:T(8,128)}, u32[]{:S(2)}, u32[]{:S(2)}) collective-permute-start(f32[16,64,128]{2,1,0:T(8,128)} %get-tuple-element.18), channel_id=1, source_target_pairs={{0,224},{32,64},{64,32},{96,128},{128,96},{160,192},{192,160},{224... | collective-permute-start | bytes 1572872 | tf_op jit(solution)/shard_map/ppermute | solution.py:20
  18.9 22.2 %all-to-all-start = ((f32[256,1,128]{2,1,0:T(1,128)}), f32[256,1,128]{2,1,0:T(1,128)}, u32[]{:S(2)}, u32[]{:S(2)}) async-start(f32[256,1,128]{2,1,0:T(1,128)} %bitcast.6), calls=%async_computation | async-start | bytes 262144 | tf_op jit(solution)/shard_map/all_to_all | solution.py:527
  29.0 3.4 %collective-permute-start.4 = (f32[128,128]{1,0:T(8,128)}, f32[128,128]{1,0:T(8,128)S(1)}, u32[]{:S(2)}, u32[]{:S(2)}) collective-permute-start(f32[128,128]{1,0:T(8,128)} %get-tuple-element.21), channel_id=1, source_target_pairs={{0,1},{1,0},{2,3},{3,2},{4,5},{5,4},{6,7},{7,6},{8,9},{9,8},{10,11... | collective-permute-start | bytes 196616 | tf_op jit(solution)/shard_map/ppermute | solution.py:20
  32.4 0.6 %copy-start.2 = (f32[128,128]{1,0:T(8,128)}, f32[128,128]{1,0:T(8,128)S(1)}, u32[]{:S(2)}) copy-start(f32[128,128]{1,0:T(8,128)S(1)} %collective-permute-done.4.gza_in) | copy-start | bytes 196612
  32.4 7.4 %collective-permute-start.5 = (f32[128,128]{1,0:T(8,128)}, f32[128,128]{1,0:T(8,128)}, u32[]{:S(2)}, u32[]{:S(2)}) collective-permute-start(f32[128,128]{1,0:T(8,128)} %get-tuple-element.22), channel_id=1, source_target_pairs={{0,3},{1,2},{2,1},{3,0},{4,7},{5,6},{6,5},{7,4},{8,11},{9,10},{10,... | collective-permute-start | bytes 196616 | tf_op jit(solution)/shard_map/ppermute | solution.py:20

commit v4 on v3

--- a/solution.py
+++ b/solution.py
@@ -391,7 +391,7 @@
             pltpu.SemaphoreType.DMA((7,)),
         ],
         compiler_params=params(20),
-        cost_estimate=cost(6 << 30, 6),
+        cost_estimate=pl.CostEstimate(flops=4 << 30, bytes_accessed=6 << 20, transcendentals=0),
         name="interior",
     )(
         in_hbm(chem), fields, in_hbm(vel), in_hbm(rate), in_hbm(sx), in_hbm(sy), in_hbm(szt)

time: 47.3 us -> 47.4 us (level)
  waiting for transfers between devices: 2.49 us -> 3.49 us
  local copies, waits for them, and re-layouts: 0.63 us -> 0.01 us
    all_to_all x1, waiting for transfers between devices: 1.36 us -> 3.47 us  [shards(): rows = lax.all_to_all(contrib, AXES, 0, 0, tiled=True)]
    all_to_all x1, starting transfers between devices: 10.1 us -> 8.43 us  [shards(): rows = lax.all_to_all(contrib, AXES, 0, 0, tiled=True)]
    ppermute x6, starting transfers between devices: 14.8 us -> 16.2 us  [swap(): return (lax.ppermute(a, axis, plan_a), lax.ppermute(b, axis, plan_b))]
    ppermute x6, waiting for transfers between devices: 1.13 us -> 0.02 us  [swap(): return (lax.ppermute(a, axis, plan_a), lax.ppermute(b, axis, plan_b))]
    unnamed x6, local copies, waits for them, and re-layouts: 0.63 us -> 0.01 us
  transfers between devices with their start and end apart: 7 -> 7, of which waited for: 2 -> 1; matrix products, arithmetic and copies ran while one was open for 0% -> 0% of each run, Pallas kernels for 20% -> 20%
where the time goes in v4:
time: 47.4 us; the launch traced here: 47.2 us
  starting transfers between devices  24.6 us (52%)
  Pallas kernels  17.6 us (37%)
  waiting for transfers between devices  3.49 us (7%)
  between operations  1.55 us (3%)
    ppermute x6, starting transfers between devices, swap(): return (lax.ppermute(a, axis, plan_a), lax.ppermute(b, axis, plan_b))  16.2 us
    all_to_all x1, starting transfers between devices, shards(): rows = lax.all_to_all(contrib, AXES, 0, 0, tiled=True)  8.43 us
    pallas_call x1, Pallas kernels, call_interior(): pl.pallas_call(interior, out_shape=(resident(nv + 2, 256, 128), resident(...  6.73 us
    pallas_call x1, Pallas kernels, call_finish(): pl.pallas_call(finish, out_shape=(jax.ShapeDtypeStruct((nv, 256, 128), f3...  5.79 us
    all_to_all x1, waiting for transfers between devices, shards(): rows = lax.all_to_all(contrib, AXES, 0, 0, tiled=True)  3.47 us
    pallas_call x1, Pallas kernels, call_pack_xz(): pl.pallas_call(pack_xz, out_shape=(gx, gx, gz, gz, jax.ShapeDtypeStruct((...  2.56 us
    pallas_call x1, Pallas kernels, call_pack_y(): pl.pallas_call(pack_y, out_shape=(gy, gy, resident(nv + 2, 256, 128)), in...  2.5 us
  transfers between devices with their start and end apart: 7, of which 1 were waited for; matrix products, arithmetic and copies ran while one was open for 0% of the time, Pallas kernels for 20%

profile of v4, /device:TPU:1, one launch (start us, length us, event | category | flops | bytes accessed | tf_op | source)
XLA Modules:
  0.0 47.2 jit_solution(12600765442592965937)
XLA Ops:
  0.6 0.0 copy-start
  0.6 0.0 copy-start.1
  0.7 2.5 %pack_y.1 = (f32[16,64,128]{2,1,0:T(8,128)}, f32[16,64,128]{2,1,0:T(8,128)}, f32[16,256,128]{2,1,0:T(8,128)S(1)}) custom-call(f32[14,256,128]{2,1,0:T(8,128)} %bitcast.13, f32[3,256,128]{2,1,0:T(8,128)} %bitcast.10, f32[256,128]{1,0:T(8,128)} %bitcast.14), custom_call_target="tpu_custom_call" | custom-call | flops 1 | bytes 1024 | tf_op jit(solution)/shard_map/pack_y/pallas_call | solution.py:101
  3.2 3.8 %collective-permute-start.2 = (f32[16,64,128]{2,1,0:T(8,128)}, f32[16,64,128]{2,1,0:T(8,128)S(1)}, u32[]{:S(2)}, u32[]{:S(2)}) collective-permute-start(f32[16,64,128]{2,1,0:T(8,128)} %get-tuple-element.19), channel_id=1, source_target_pairs={{0,4},{4,0},{8,12},{12,8},{16,20},{20,16},{24,28},{28,24},{1,5},{5... | collective-permute-start | bytes 1572872 | tf_op jit(solution)/shard_map/ppermute | solution.py:20
  7.0 2.3 %collective-permute-start.3 = (f32[16,64,128]{2,1,0:T(8,128)}, f32[16,64,128]{2,1,0:T(8,128)}, u32[]{:S(2)}, u32[]{:S(2)}) collective-permute-start(f32[16,64,128]{2,1,0:T(8,128)} %get-tuple-element.20), channel_id=1, source_target_pairs={{0,28},{4,8},{8,4},{12,16},{16,12},{20,24},{24,20},{28,0},{1,29},{... | collective-permute-start | bytes 1572872 | tf_op jit(solution)/shard_map/ppermute | solution.py:20
  9.9 0.0 copy-done
  9.9 0.0 copy-done.1
  10.0 2.6 %pack_xz.1 = (f32[16,64,128]{2,1,0:T(8,128)}, f32[16,64,128]{2,1,0:T(8,128)}, f32[128,128]{1,0:T(8,128)}, f32[128,128]{1,0:T(8,128)}, f32[256,128]{1,0:T(8,128)}) custom-call(s32[1,1,1]{2,1,0:T(1,128)S(6)} %copy.15.ids, f32[16,256,128]{2,1,0:T(8,128)S(1)} %get-tuple-element.14.fields, f32[3,256,128]{2,1,0:T(8,128)S(1)} %bitcast.12, f32[128,16,128]{2,1,0:T(8,128)S(1)} %copy-done.1), custom_call_target="tpu_custom_call" | custom-call | flops 1 | bytes 1024 | tf_op jit(solution)/shard_map/pack_xz/pallas_call | solution.py:174
  12.5 1.7 %collective-permute-start = (f32[16,64,128]{2,1,0:T(8,128)}, f32[16,64,128]{2,1,0:T(8,128)}, u32[]{:S(2)}, u32[]{:S(2)}) collective-permute-start(f32[16,64,128]{2,1,0:T(8,128)} %get-tuple-element.17), channel_id=1, source_target_pairs={{0,32},{32,0},{64,96},{96,64},{128,160},{160,128},{192,224},{224,1... | collective-permute-start | bytes 1572872 | tf_op jit(solution)/shard_map/ppermute | solution.py:20
  14.3 4.7 %collective-permute-start.1 = (f32[16,64,128]{2,1,0:T(8,128)}, f32[16,64,128]{2,1,0:T(8,128)}, u32[]{:S(2)}, u32[]{:S(2)}) collective-permute-start(f32[16,64,128]{2,1,0:T(8,128)} %get-tuple-element.18), channel_id=1, source_target_pairs={{0,224},{32,64},{64,32},{96,128},{128,96},{160,192},{192,160},{224... | collective-permute-start | bytes 1572872 | tf_op jit(solution)/shard_map/ppermute | solution.py:20
  18.9 1.8 %collective-permute-start.4 = (f32[128,128]{1,0:T(8,128)}, f32[128,128]{1,0:T(8,128)S(1)}, u32[]{:S(2)}, u32[]{:S(2)}) collective-permute-start(f32[128,128]{1,0:T(8,128)} %get-tuple-element.21), channel_id=1, source_target_pairs={{0,1},{1,0},{2,3},{3,2},{4,5},{5,4},{6,7},{7,6},{8,9},{9,8},{10,11... | collective-permute-start | bytes 196616 | tf_op jit(solution)/shard_map/ppermute | solution.py:20
  20.7 8.4 %all-to-all-start = ((f32[256,1,128]{2,1,0:T(1,128)}), f32[256,1,128]{2,1,0:T(1,128)}, u32[]{:S(2)}, u32[]{:S(2)}) async-start(f32[256,1,128]{2,1,0:T(1,128)} %bitcast.6), calls=%async_computation | async-start | bytes 262144 | tf_op jit(solution)/shard_map/all_to_all | solution.py:527
  29.1 0.0 collective-permute-done.4.gza_in
  29.1 0.0 copy-start.2
  29.1 1.9 %collective-permute-start.5 = (f32[128,128]{1,0:T(8,128)}, f32[128,128]{1,0:T(8,128)}, u32[]{:S(2)}, u32[]{:S(2)}) collective-permute-start(f32[128,128]{1,0:T(8,128)} %get-tuple-element.22), channel_id=1, source_target_pairs={{0,3},{1,2},{2,1},{3,0},{4,7},{5,6},{6,5},{7,4},{8,11},{9,10},{10,... | collective-permute-start | bytes 196616 | tf_op jit(solution)/shard_map/ppermute | solution.py:20
  31.0 0.0 copy-done.2
  31.0 6.7 %interior.1 = (f32[16,256,128]{2,1,0:T(8,128)S(1)}, bf16[256,1792]{1,0:T(8,128)(2,1)S(1)}) custom-call(f32[14,14]{1,0:T(8,128)} %chem_in.1, f32[16,256,128]{2,1,0:T(8,128)S(1)} %get-tuple-element.14.fields, f32[3,256,128]{2,1,0:T(8,128)} %bitcast.11, f32[256,128]{1,0:T(8,128)} %bitcast.17, f32[2,16,24]{2,1,0:T(8,128)} %sx_in.1, ...), custom_call_target="tpu_custom_call", output_to_operand_aliasing={{0}: (1, {})} | custom-call | flops 4294967296 | bytes 6291456 | tf_op jit(solution)/shard_map/interior/pallas_call | solution.py:370
  37.8 0.0 collective-permute-done.5.gzb_in
  37.8 3.5 %all-to-all-done = f32[256,1,128]{2,1,0:T(1,128)} async-done(((f32[256,1,128]{2,1,0:T(1,128)}), f32[256,1,128]{2,1,0:T(1,128)}, u32[]{:S(2)}, u32[]{:S(2)}) %all-to-all-start) | async-done | bytes 131104 | tf_op jit(solution)/shard_map/all_to_all | solution.py:527
  41.3 0.0 collective-permute-done.2.gya_in
  41.3 0.0 collective-permute-done.3.gyb_in
  41.3 0.0 collective-permute-done.gxa_in
  41.3 0.0 collective-permute-done.1.gxb_in
  41.3 5.8 %finish.1 = (f32[14,256,128]{2,1,0:T(8,128)}, f32[1,128]{1,0:T(1,128)}) custom-call(f32[16,256,128]{2,1,0:T(8,128)S(1)} %get-tuple-element.15.base, bf16[256,1792]{1,0:T(8,128)(2,1)S(1)} %get-tuple-element.16.edge, f32[16,64,128]{2,1,0:T(8,128)} %collective-permute-done.gxa_in, f32[16,64,128]{2,1,0:T(8,128)} %collective-permute-done.1.gxb_in, ...), custom_call_target="tpu_custom_call" | custom-call | flops 1 | bytes 1024 | tf_op jit(solution)/shard_map/finish/pallas_call | solution.py:478
Async XLA Ops:
  0.6 9.3 %copy-start = (f32[3,16,16,128]{3,2,1,0:T(8,128)S(1)}, f32[3,16,16,128]{3,2,1,0:T(8,128)}, u32[]{:S(2)}) copy-start(f32[3,16,16,128]{3,2,1,0:T(8,128)} %param.11) | copy-start | bytes 1179652
  0.6 9.3 %copy-start.1 = (f32[128,16,128]{2,1,0:T(8,128)S(1)}, f32[128,16,128]{2,1,0:T(8,128)}, u32[]{:S(2)}) copy-start(f32[128,16,128]{2,1,0:T(8,128)} %sens.1) | copy-start | bytes 3145732
  3.2 38.1 %collective-permute-start.2 = (f32[16,64,128]{2,1,0:T(8,128)}, f32[16,64,128]{2,1,0:T(8,128)S(1)}, u32[]{:S(2)}, u32[]{:S(2)}) collective-permute-start(f32[16,64,128]{2,1,0:T(8,128)} %get-tuple-element.19), channel_id=1, source_target_pairs={{0,4},{4,0},{8,12},{12,8},{16,20},{20,16},{24,28},{28,24},{1,5},{5... | collective-permute-start | bytes 1572872 | tf_op jit(solution)/shard_map/ppermute | solution.py:20
  7.0 34.3 %collective-permute-start.3 = (f32[16,64,128]{2,1,0:T(8,128)}, f32[16,64,128]{2,1,0:T(8,128)}, u32[]{:S(2)}, u32[]{:S(2)}) collective-permute-start(f32[16,64,128]{2,1,0:T(8,128)} %get-tuple-element.20), channel_id=1, source_target_pairs={{0,28},{4,8},{8,4},{12,16},{16,12},{20,24},{24,20},{28,0},{1,29},{... | collective-permute-start | bytes 1572872 | tf_op jit(solution)/shard_map/ppermute | solution.py:20
  12.5 28.7 %collective-permute-start = (f32[16,64,128]{2,1,0:T(8,128)}, f32[16,64,128]{2,1,0:T(8,128)}, u32[]{:S(2)}, u32[]{:S(2)}) collective-permute-start(f32[16,64,128]{2,1,0:T(8,128)} %get-tuple-element.17), channel_id=1, source_target_pairs={{0,32},{32,0},{64,96},{96,64},{128,160},{160,128},{192,224},{224,1... | collective-permute-start | bytes 1572872 | tf_op jit(solution)/shard_map/ppermute | solution.py:20
  14.3 27.0 %collective-permute-start.1 = (f32[16,64,128]{2,1,0:T(8,128)}, f32[16,64,128]{2,1,0:T(8,128)}, u32[]{:S(2)}, u32[]{:S(2)}) collective-permute-start(f32[16,64,128]{2,1,0:T(8,128)} %get-tuple-element.18), channel_id=1, source_target_pairs={{0,224},{32,64},{64,32},{96,128},{128,96},{160,192},{192,160},{224... | collective-permute-start | bytes 1572872 | tf_op jit(solution)/shard_map/ppermute | solution.py:20
  18.9 10.2 %collective-permute-start.4 = (f32[128,128]{1,0:T(8,128)}, f32[128,128]{1,0:T(8,128)S(1)}, u32[]{:S(2)}, u32[]{:S(2)}) collective-permute-start(f32[128,128]{1,0:T(8,128)} %get-tuple-element.21), channel_id=1, source_target_pairs={{0,1},{1,0},{2,3},{3,2},{4,5},{5,4},{6,7},{7,6},{8,9},{9,8},{10,11... | collective-permute-start | bytes 196616 | tf_op jit(solution)/shard_map/ppermute | solution.py:20
  20.7 20.6 %all-to-all-start = ((f32[256,1,128]{2,1,0:T(1,128)}), f32[256,1,128]{2,1,0:T(1,128)}, u32[]{:S(2)}, u32[]{:S(2)}) async-start(f32[256,1,128]{2,1,0:T(1,128)} %bitcast.6), calls=%async_computation | async-start | bytes 262144 | tf_op jit(solution)/shard_map/all_to_all | solution.py:527
  29.1 1.9 %copy-start.2 = (f32[128,128]{1,0:T(8,128)}, f32[128,128]{1,0:T(8,128)S(1)}, u32[]{:S(2)}) copy-start(f32[128,128]{1,0:T(8,128)S(1)} %collective-permute-done.4.gza_in) | copy-start | bytes 196612
  29.1 8.6 %collective-permute-start.5 = (f32[128,128]{1,0:T(8,128)}, f32[128,128]{1,0:T(8,128)}, u32[]{:S(2)}, u32[]{:S(2)}) collective-permute-start(f32[128,128]{1,0:T(8,128)} %get-tuple-element.22), channel_id=1, source_target_pairs={{0,3},{1,2},{2,1},{3,0},{4,7},{5,6},{6,5},{7,4},{8,11},{9,10},{10,... | collective-permute-start | bytes 196616 | tf_op jit(solution)/shard_map/ppermute | solution.py:20
